TPU v7x, 32 devices: a whole 2x2x4 slice. The times are simulated.
32 devices in a mesh: group: 4 (over z_hi, core), blk: 4 (over y, x), head: 2 (over z_lo).
Axes of the slice: x: 2, y: 2, z: 4 (z_hi: 2, z_lo: 2; z = z_hi * 2 + z_lo), core: 2. Of those that a mesh axis runs over, the one named last changes fastest.
Arguments:
- tokens: bfloat16 [8, 1024, 1024], P('group', ('blk', 'head')), may hold values from -6 to 6
- segments: int32 [8, 1024], P('group'), may hold values from 0 to 7, never falling along the last dimension, each value on 1 to 512 neighbouring positions
- routes: int32 [8, 1024, 8], P('group', ('blk', 'head')), may hold values from 0 to 31, all different within a row; in each aligned block of 128 rows (0 to 127, 128 to 255, ..., all dimensions but the last counted through in order) at most 36 rows name the same one
- cotangent: bfloat16 [8, 1024, 1024], P('group', ('blk', 'head')), may hold values from -6 to 6
- attn_gain: bfloat16 [1024], P(('blk', 'head')), may hold values from 0.5 to 1.5
- moe_gain: bfloat16 [1024], P(('blk', 'head')), may hold values from 0.5 to 1.5
- query_weight: bfloat16 [1024, 1024], P(('blk', 'head')), may hold values from -0.1875 to 0.1875
- key_projection_matrix: bfloat16 [1024, 512], P(('blk', 'head')), may hold values from -0.1875 to 0.1875
- value_projection_matrix: bfloat16 [1024, 512], P(('blk', 'head')), may hold values from -0.1875 to 0.1875
- out_weight: bfloat16 [1024, 1024], P(('blk', 'head')), may hold values from -1.5 to 1.5
- router_weight: bfloat16 [1024, 32], P(('blk', 'head')), may hold values from -0.375 to 0.375
- gate_weight: bfloat16 [32, 1024, 512], P(('blk', 'head')), may hold values from -0.1875 to 0.1875
- up_weight: bfloat16 [32, 1024, 512], P(('blk', 'head')), may hold values from -0.1875 to 0.1875
- down_weight: bfloat16 [32, 512, 1024], P(('blk', 'head')), may hold values from -0.75 to 0.75
Outputs:
- mixed: bfloat16 [8, 1024, 1024], P('group', ('blk', 'head'))
- token_grad: float32 [8, 1024, 1024], P('group', ('blk', 'head'))
- attn_gain_grad: float32 [1024], P(('blk', 'head'))
- moe_gain_grad: float32 [1024], P(('blk', 'head'))
- query_weight_grad: float32 [1024, 1024], P(('blk', 'head'))
- key_weight_grad: float32 [1024, 512], P(('blk', 'head'))
- value_weight_grad: float32 [1024, 512], P(('blk', 'head'))
- out_weight_grad: float32 [1024, 1024], P(('blk', 'head'))
- router_weight_grad: float32 [1024, 32], P(('blk', 'head'))
- gate_weight_grad: float32 [32, 1024, 512], P(('blk', 'head'))
- up_weight_grad: float32 [32, 1024, 512], P(('blk', 'head'))
- down_weight_grad: float32 [32, 512, 1024], P(('blk', 'head'))
Inputs may be any that keep to these rules, and one draw needn't show every extreme that they name: `routes`: each row names 8 distinct experts; in each aligned block of 128 positions of a sequence no expert is named by more than 36 rows, a bound that some block reaches. `segments`: within each sequence the numbers never fall; each document has at most 512 positions, and one has exactly 512.
All inputs are finite; a program needn't handle non-finite values.
Results may differ from a plain program's by a relative error of at most 0.03.
Values may be sent and summed in bfloat16 or wider, within the bound.
A program may use at most 192 MiB of HBM per device.

v0:
```python
import jax
import jax.numpy as jnp
from jax import lax
from jax.sharding import PartitionSpec as P

QUERY_HEADS = 16
KEY_VALUE_HEADS = 8
HEAD_SIZE = 64
TOP = 8
CAPH = 36


epsilon = 1e-05
rope_base = 10000.0
masked_out = -1e30
key_block = 512


def rms_norm(values, gain_vec):
    return values * lax.rsqrt(jnp.mean(values * values, -1, keepdims=True) + epsilon) * gain_vec


def rotary_embedding(field_vals, places, turn_sign):
    half_dim = field_vals.shape[-1] // 2
    frequency = rope_base ** (-jnp.arange(half_dim, dtype=jnp.float32) * 2.0 / field_vals.shape[-1])
    angles = places.astype(jnp.float32)[:, None] * frequency[None, :]
    cosine = jnp.cos(angles)[:, None, :]
    sine_vals = turn_sign * jnp.sin(angles)[:, None, :]
    first_half = field_vals[..., :half_dim]
    second = field_vals[..., half_dim:]
    return jnp.concatenate(
        [first_half * cosine - second * sine_vals, second * cosine + first_half * sine_vals], -1
    )


def add_rows(running, addend, row_start):
    current = lax.dynamic_slice_in_dim(running, row_start, addend.shape[1], 1)
    return lax.dynamic_update_slice_in_dim(running, current + addend, row_start, 1)


def on_device(
    tokens,
    segments,
    routes,
    cotangent,
    attn_gain,
    moe_gain,
    query_weight,
    key_projection_matrix,
    value_projection_matrix,
    out_weight,
    router_weight,
    gate_weight,
    up_weight,
    down_weight,
):
    head_groups, number_of_rows, width_dim = tokens.shape
    query_per_key_head = QUERY_HEADS // KEY_VALUE_HEADS
    shared_head_count = lax.axis_size("head")
    query_rows = number_of_rows * shared_head_count
    grouped_keys = KEY_VALUE_HEADS // shared_head_count
    scale_val = HEAD_SIZE ** (-0.5)
    number_of_tokens = head_groups * number_of_rows
    seq_length = lax.axis_size("blk") * query_rows
    cycle_index = lax.axis_index("blk")
    local_placement = (
        cycle_index * shared_head_count + lax.axis_index("head")
    ) * number_of_rows + jnp.arange(number_of_rows, dtype=jnp.int32)
    own_start = cycle_index * query_rows
    query_place = own_start + jnp.arange(query_rows, dtype=jnp.int32)
    query_doc = lax.dynamic_slice_in_dim(segments, own_start, query_rows, 1)
    query_full, key_full, value_full, out_full, router_full, gain_attn, gain_moe = (
        lax.all_gather(query_weight, ("blk", "head"), axis=0, tiled=True),
        lax.all_gather(key_projection_matrix, ("blk", "head"), axis=0, tiled=True),
        lax.all_gather(value_projection_matrix, ("blk", "head"), axis=0, tiled=True),
        lax.all_gather(out_weight, ("blk", "head"), axis=0, tiled=True),
        lax.all_gather(router_weight, ("blk", "head"), axis=0, tiled=True),
        lax.all_gather(attn_gain, ("blk", "head"), axis=0, tiled=True),
        lax.all_gather(moe_gain, ("blk", "head"), axis=0, tiled=True),
    )
    flat_rows = tokens.reshape(number_of_tokens, width_dim).astype(jnp.float32)
    attn_normed, attn_pull = jax.vjp(rms_norm, flat_rows, gain_attn.astype(jnp.float32))
    attn_in = attn_normed.astype(jnp.bfloat16)
    query_pre = jnp.dot(attn_in, query_full, preferred_element_type=jnp.float32)
    key_before_rotary = jnp.dot(attn_in, key_full, preferred_element_type=jnp.float32)
    value_low = (
        jnp.dot(attn_in, value_full, preferred_element_type=jnp.float32)
        .astype(jnp.bfloat16)
        .reshape(head_groups, number_of_rows, KEY_VALUE_HEADS * HEAD_SIZE)
    )
    query_low = (
        rotary_embedding(
            query_pre.reshape(head_groups, number_of_rows, QUERY_HEADS, HEAD_SIZE),
            local_placement,
            1.0,
        )
        .astype(jnp.bfloat16)
        .reshape(head_groups, number_of_rows, QUERY_HEADS * HEAD_SIZE)
    )
    key_low = (
        rotary_embedding(
            key_before_rotary.reshape(head_groups, number_of_rows, KEY_VALUE_HEADS, HEAD_SIZE),
            local_placement,
            1.0,
        )
        .astype(jnp.bfloat16)
        .reshape(head_groups, number_of_rows, KEY_VALUE_HEADS * HEAD_SIZE)
    )
    query_split, key_split, value_split = (
        lax.all_to_all(query_low, "head", split_axis=2, concat_axis=1, tiled=True),
        lax.all_to_all(key_low, "head", split_axis=2, concat_axis=1, tiled=True),
        lax.all_to_all(value_low, "head", split_axis=2, concat_axis=1, tiled=True),
    )
    query_vectors = query_split.reshape(
        head_groups, query_rows, grouped_keys, query_per_key_head, HEAD_SIZE
    )

    def key_view(source, offset, sub_rows):
        return lax.dynamic_slice_in_dim(source, offset, sub_rows, 1).reshape(
            head_groups, sub_rows, grouped_keys, HEAD_SIZE
        )

    def scored_at(query_part, key_row_block, q_place, q_doc, key_start, sub_rows):
        raw_scores = (
            jnp.einsum(
                "bqgrd,bkgd->bqgrk", query_part, key_row_block, preferred_element_type=jnp.float32
            )
            * scale_val
        )
        key_place = key_start + jnp.arange(sub_rows, dtype=jnp.int32)
        key_doc = lax.dynamic_slice_in_dim(segments, key_start, sub_rows, 1)
        allowed = (q_place[None, :, None] >= key_place[None, None, :]) & (
            q_doc[:, :, None] == key_doc[:, None, :]
        )
        return (raw_scores, allowed[:, :, None, None, :])

    def scored(key_row_block, key_start, sub_rows):
        return scored_at(query_vectors, key_row_block, query_place, query_doc, key_start, sub_rows)

    stats_shape = (head_groups, query_rows, grouped_keys, query_per_key_head)
    init_state = (
        jnp.full(stats_shape, masked_out, jnp.float32),
        jnp.zeros(stats_shape, jnp.float32),
        jnp.zeros(stats_shape + (HEAD_SIZE,), jnp.float32),
    )
    key_all, value_all = (
        lax.all_gather(key_split, "blk", axis=1, tiled=True),
        lax.all_gather(value_split, "blk", axis=1, tiled=True),
    )
    fold_state = init_state
    total_rows = key_all.shape[1]
    sub_rows = key_block

    def forward_one_block(block_state, block_index):
        offset = block_index * sub_rows
        key_row_block = key_view(key_all, offset, sub_rows)
        value_row_block = key_view(value_all, offset, sub_rows)
        raw_scores, allowed = scored(key_row_block, 0 + offset, sub_rows)
        running_max, running_sum, running_acc = block_state
        masked = jnp.where(allowed, raw_scores, masked_out)
        new_max = jnp.maximum(running_max, jnp.max(masked, -1))
        shrink = jnp.exp(running_max - new_max)
        weights_soft = jnp.where(allowed, jnp.exp(masked - new_max[..., None]), 0.0)
        new_sum = running_sum * shrink + jnp.sum(weights_soft, -1)
        new_acc = running_acc * shrink[..., None] + jnp.einsum(
            "bqgrk,bkgd->bqgrd",
            weights_soft.astype(jnp.bfloat16),
            value_row_block,
            preferred_element_type=jnp.float32,
        )
        return ((new_max, new_sum, new_acc), None)

    fold_state, unused = lax.scan(
        forward_one_block, fold_state, jnp.arange(total_rows // sub_rows, dtype=jnp.int32)
    )
    running_max, running_sum, running_acc = fold_state
    mix_heads = running_acc / running_sum[..., None]
    log_total = running_max + jnp.log(running_sum)
    mix_low = mix_heads.astype(jnp.bfloat16).reshape(
        head_groups, query_rows, grouped_keys * query_per_key_head * HEAD_SIZE
    )
    mix_tokens = lax.all_to_all(mix_low, "head", split_axis=1, concat_axis=2, tiled=True)
    attn_mix = mix_tokens.reshape(number_of_tokens, QUERY_HEADS * HEAD_SIZE)
    residual = flat_rows + jnp.dot(attn_mix, out_full, preferred_element_type=jnp.float32)
    moe_normed, moe_pull = jax.vjp(rms_norm, residual, gain_moe.astype(jnp.float32))
    moe_in = moe_normed.astype(jnp.bfloat16)
    logits = jnp.dot(moe_in, router_full, preferred_element_type=jnp.float32)
    route_flat = routes.reshape(number_of_tokens, TOP)
    experts_all = router_full.shape[1]
    choose = route_flat[:, :, None] == jnp.arange(experts_all, dtype=jnp.int32)[None, None, :]
    choose_float = choose.astype(jnp.float32)
    picked_logits = jnp.einsum("nke,ne->nk", choose_float, logits)
    route_weights = jax.nn.softmax(picked_logits, axis=-1)
    choose_whole = choose.astype(jnp.int32).reshape(head_groups, number_of_rows * TOP, experts_all)
    slot_rank = jnp.sum(jnp.cumsum(choose_whole, 1) * choose_whole, -1) - 1
    slot_index = (slot_rank + jnp.arange(head_groups, dtype=jnp.int32)[:, None] * CAPH).reshape(-1)
    targets = route_flat.reshape(-1)
    lane_count = head_groups * CAPH
    outgoing = (
        jnp.zeros((experts_all, lane_count, width_dim), jnp.bfloat16)
        .at[targets, slot_index]
        .set(jnp.repeat(moe_in, TOP, axis=0))
    )
    arrived = lax.all_to_all(outgoing, ("blk", "head"), split_axis=0, concat_axis=1, tiled=True)
    gate_val = jnp.einsum("end,edf->enf", arrived, gate_weight, preferred_element_type=jnp.float32)
    up_val = jnp.einsum("end,edf->enf", arrived, up_weight, preferred_element_type=jnp.float32)
    hidden_low = (jax.nn.silu(gate_val) * up_val).astype(jnp.bfloat16)
    expert_out = jnp.einsum(
        "enf,efd->end", hidden_low, down_weight, preferred_element_type=jnp.float32
    ).astype(jnp.bfloat16)
    returned = lax.all_to_all(expert_out, ("blk", "head"), split_axis=1, concat_axis=0, tiled=True)
    picked_rows = returned[targets, slot_index].reshape(number_of_tokens, TOP, width_dim)
    moe_out = jnp.einsum(
        "nk,nkd->nd", route_weights, picked_rows, preferred_element_type=jnp.float32
    )
    mixed = (
        (residual + moe_out).astype(jnp.bfloat16).reshape(head_groups, number_of_rows, width_dim)
    )
    grad_full = cotangent.reshape(number_of_tokens, width_dim).astype(jnp.float32)
    weight_grad = jnp.einsum(
        "nkd,nd->nk", picked_rows, grad_full, preferred_element_type=jnp.float32
    )
    pair_grad = (
        (route_weights[:, :, None] * grad_full[:, None, :])
        .astype(jnp.bfloat16)
        .reshape(number_of_tokens * TOP, width_dim)
    )
    grad_outgoing = jnp.zeros_like(outgoing).at[targets, slot_index].set(pair_grad)
    grad_arrived = lax.all_to_all(
        grad_outgoing, ("blk", "head"), split_axis=0, concat_axis=1, tiled=True
    )
    grad_hidden = jnp.einsum(
        "end,efd->enf", grad_arrived, down_weight, preferred_element_type=jnp.float32
    )
    sigmoid_val = jax.nn.sigmoid(gate_val)
    grad_gate = (
        grad_hidden * up_val * sigmoid_val * (1.0 + gate_val * (1.0 - sigmoid_val))
    ).astype(jnp.bfloat16)
    grad_up = (grad_hidden * gate_val * sigmoid_val).astype(jnp.bfloat16)
    down_weight_grad = jnp.einsum(
        "enf,end->efd", hidden_low, grad_arrived, preferred_element_type=jnp.float32
    )
    gate_weight_grad = jnp.einsum(
        "end,enf->edf", arrived, grad_gate, preferred_element_type=jnp.float32
    )
    up_weight_grad = jnp.einsum(
        "end,enf->edf", arrived, grad_up, preferred_element_type=jnp.float32
    )
    pair_back = (
        jnp.einsum("enf,edf->end", grad_gate, gate_weight, preferred_element_type=jnp.float32)
        + jnp.einsum("enf,edf->end", grad_up, up_weight, preferred_element_type=jnp.float32)
    ).astype(jnp.bfloat16)
    grad_returned = lax.all_to_all(
        pair_back, ("blk", "head"), split_axis=1, concat_axis=0, tiled=True
    )
    moe_in_grad = jnp.sum(
        grad_returned[targets, slot_index].reshape(number_of_tokens, TOP, width_dim),
        axis=1,
        dtype=jnp.float32,
    )
    mean_term = jnp.sum(route_weights * weight_grad, -1, keepdims=True)
    logit_grad = jnp.einsum("nk,nke->ne", route_weights * (weight_grad - mean_term), choose_float)
    router_grad = jnp.dot(moe_in.T, logit_grad, preferred_element_type=jnp.float32)
    moe_in_grad = moe_in_grad + jnp.dot(
        logit_grad, router_full.T, preferred_element_type=jnp.float32
    )
    residual_part, moe_gain_grad = moe_pull(moe_in_grad)
    residual_grad = grad_full + residual_part
    out_grad_low = residual_grad.astype(jnp.bfloat16)
    out_weight_grad = jnp.dot(attn_mix.T, out_grad_low, preferred_element_type=jnp.float32)
    mix_grad = (
        jnp.dot(out_grad_low, out_full.T, preferred_element_type=jnp.float32)
        .astype(jnp.bfloat16)
        .reshape(head_groups, number_of_rows, QUERY_HEADS * HEAD_SIZE)
    )
    mix_grad_heads = lax.all_to_all(
        mix_grad, "head", split_axis=2, concat_axis=1, tiled=True
    ).reshape(head_groups, query_rows, grouped_keys, query_per_key_head, HEAD_SIZE)
    delta_term = jnp.sum(mix_grad_heads.astype(jnp.float32) * mix_heads, -1)
    query_zero = jnp.zeros(stats_shape + (HEAD_SIZE,), jnp.float32)
    back_init = (
        query_zero,
        jnp.zeros((head_groups, seq_length, grouped_keys, HEAD_SIZE), jnp.float32),
        jnp.zeros((head_groups, seq_length, grouped_keys, HEAD_SIZE), jnp.float32),
    )
    fold_state = back_init
    total_rows = key_all.shape[1]

    def backward_one_block(block_state, block_index):
        offset = block_index * key_block
        key_start = 0 + offset
        key_row_block = key_view(key_all, offset, key_block)
        value_row_block = key_view(value_all, offset, key_block)
        raw_scores, allowed = scored(key_row_block, key_start, key_block)
        masked = jnp.where(allowed, raw_scores, masked_out)
        probability = jnp.where(allowed, jnp.exp(masked - log_total[..., None]), 0.0)
        prob_grad = jnp.einsum(
            "bqgrd,bkgd->bqgrk", mix_grad_heads, value_row_block, preferred_element_type=jnp.float32
        )
        score_grad = (probability * (prob_grad - delta_term[..., None]) * scale_val).astype(
            jnp.bfloat16
        )
        grad_query = block_state[0] + jnp.einsum(
            "bqgrk,bkgd->bqgrd", score_grad, key_row_block, preferred_element_type=jnp.float32
        )
        value_part_grad = jnp.einsum(
            "bqgrk,bqgrd->bkgd",
            probability.astype(jnp.bfloat16),
            mix_grad_heads,
            preferred_element_type=jnp.float32,
        )
        key_part_grad = jnp.einsum(
            "bqgrk,bqgrd->bkgd", score_grad, query_vectors, preferred_element_type=jnp.float32
        )
        grad_keys = add_rows(block_state[1], key_part_grad, key_start)
        grad_values = add_rows(block_state[2], value_part_grad, key_start)
        return ((grad_query, grad_keys, grad_values), None)

    fold_state, unused = lax.scan(
        backward_one_block, fold_state, jnp.arange(total_rows // key_block, dtype=jnp.int32)
    )
    grad_query, grad_keys, grad_values = fold_state
    key_own, value_own = (
        lax.psum_scatter(
            grad_keys.reshape(head_groups, seq_length, grouped_keys * HEAD_SIZE).astype(
                jnp.bfloat16
            ),
            "blk",
            scatter_dimension=1,
            tiled=True,
        ).astype(jnp.float32),
        lax.psum_scatter(
            grad_values.reshape(head_groups, seq_length, grouped_keys * HEAD_SIZE).astype(
                jnp.bfloat16
            ),
            "blk",
            scatter_dimension=1,
            tiled=True,
        ).astype(jnp.float32),
    )
    query_grad_low = (
        rotary_embedding(
            grad_query.reshape(
                head_groups, query_rows, grouped_keys * query_per_key_head, HEAD_SIZE
            ),
            query_place,
            -1.0,
        )
        .astype(jnp.bfloat16)
        .reshape(head_groups, query_rows, grouped_keys * query_per_key_head * HEAD_SIZE)
    )
    key_grad_low = (
        rotary_embedding(
            key_own.reshape(head_groups, query_rows, grouped_keys, HEAD_SIZE), query_place, -1.0
        )
        .astype(jnp.bfloat16)
        .reshape(head_groups, query_rows, grouped_keys * HEAD_SIZE)
    )
    value_grad_low = value_own.astype(jnp.bfloat16)
    query_back, key_pullback, value_pullback = (
        lax.all_to_all(query_grad_low, "head", split_axis=1, concat_axis=2, tiled=True),
        lax.all_to_all(key_grad_low, "head", split_axis=1, concat_axis=2, tiled=True),
        lax.all_to_all(value_grad_low, "head", split_axis=1, concat_axis=2, tiled=True),
    )
    query_flat = query_back.reshape(number_of_tokens, QUERY_HEADS * HEAD_SIZE)
    flattened_keys = key_pullback.reshape(number_of_tokens, KEY_VALUE_HEADS * HEAD_SIZE)
    flattened_values = value_pullback.reshape(number_of_tokens, KEY_VALUE_HEADS * HEAD_SIZE)
    query_weight_grad = jnp.dot(attn_in.T, query_flat, preferred_element_type=jnp.float32)
    key_weight_grad = jnp.dot(attn_in.T, flattened_keys, preferred_element_type=jnp.float32)
    value_weight_grad = jnp.dot(attn_in.T, flattened_values, preferred_element_type=jnp.float32)
    attn_in_grad = (
        jnp.dot(query_flat, query_full.T, preferred_element_type=jnp.float32)
        + jnp.dot(flattened_keys, key_full.T, preferred_element_type=jnp.float32)
        + jnp.dot(flattened_values, value_full.T, preferred_element_type=jnp.float32)
    )
    input_part, attn_gain_grad = attn_pull(attn_in_grad)
    token_grad = (residual_grad + input_part).reshape(head_groups, number_of_rows, width_dim)
    (
        query_shard,
        key_shard,
        value_shard,
        out_shard,
        router_shard,
        attn_gain_shard,
        moe_gain_shard,
    ) = (
        lax.psum_scatter(
            query_weight_grad.astype(jnp.bfloat16), ("blk", "head"), scatter_dimension=0, tiled=True
        ).astype(jnp.float32),
        lax.psum_scatter(
            key_weight_grad.astype(jnp.bfloat16), ("blk", "head"), scatter_dimension=0, tiled=True
        ).astype(jnp.float32),
        lax.psum_scatter(
            value_weight_grad.astype(jnp.bfloat16), ("blk", "head"), scatter_dimension=0, tiled=True
        ).astype(jnp.float32),
        lax.psum_scatter(
            out_weight_grad.astype(jnp.bfloat16), ("blk", "head"), scatter_dimension=0, tiled=True
        ).astype(jnp.float32),
        lax.psum_scatter(
            router_grad.astype(jnp.bfloat16), ("blk", "head"), scatter_dimension=0, tiled=True
        ).astype(jnp.float32),
        lax.psum_scatter(
            attn_gain_grad.astype(jnp.bfloat16), ("blk", "head"), scatter_dimension=0, tiled=True
        ).astype(jnp.float32),
        lax.psum_scatter(
            moe_gain_grad.astype(jnp.bfloat16), ("blk", "head"), scatter_dimension=0, tiled=True
        ).astype(jnp.float32),
    )
    summed = (
        lax.psum(query_shard.astype(jnp.bfloat16), "group").astype(jnp.float32),
        lax.psum(key_shard.astype(jnp.bfloat16), "group").astype(jnp.float32),
        lax.psum(value_shard.astype(jnp.bfloat16), "group").astype(jnp.float32),
        lax.psum(out_shard.astype(jnp.bfloat16), "group").astype(jnp.float32),
        lax.psum(router_shard.astype(jnp.bfloat16), "group").astype(jnp.float32),
        lax.psum(attn_gain_shard.astype(jnp.bfloat16), "group").astype(jnp.float32),
        lax.psum(moe_gain_shard.astype(jnp.bfloat16), "group").astype(jnp.float32),
        lax.psum(gate_weight_grad.astype(jnp.bfloat16), "group").astype(jnp.float32),
        lax.psum(up_weight_grad.astype(jnp.bfloat16), "group").astype(jnp.float32),
        lax.psum(down_weight_grad.astype(jnp.bfloat16), "group").astype(jnp.float32),
    )
    return (
        mixed,
        token_grad,
        summed[5],
        summed[6],
        summed[0],
        summed[1],
        summed[2],
        summed[3],
        summed[4],
        summed[7],
        summed[8],
        summed[9],
    )


def solution(mesh):
    placed = (
        P("group", ("blk", "head"), None),
        P("group", None),
        P("group", ("blk", "head"), None),
        P("group", ("blk", "head"), None),
        P(("blk", "head")),
        P(("blk", "head")),
        P(("blk", "head"), None),
        P(("blk", "head"), None),
        P(("blk", "head"), None),
        P(("blk", "head"), None),
        P(("blk", "head"), None),
        P(("blk", "head"), None, None),
        P(("blk", "head"), None, None),
        P(("blk", "head"), None, None),
    )
    return jax.shard_map(
        on_device,
        mesh=mesh,
        in_specs=placed,
        out_specs=(
            P("group", ("blk", "head"), None),
            P("group", ("blk", "head"), None),
            P(("blk", "head")),
            P(("blk", "head")),
            P(("blk", "head"), None),
            P(("blk", "head"), None),
            P(("blk", "head"), None),
            P(("blk", "head"), None),
            P(("blk", "head"), None),
            P(("blk", "head"), None, None),
            P(("blk", "head"), None, None),
            P(("blk", "head"), None, None),
        ),
        check_vma=False,
    )
```

profile of v0, /device:TPU:0, one launch (start us, length us, event | category | flops | bytes accessed | tf_op | source)
XLA Modules:
  0.0 1505.8 jit_solution(10606779024771881954)
XLA Ops:
  9.4 19.4 %all-gather = bf16[8,1,128]{2,1,0:T(2,128)(2,1)S(1)} all-gather(bf16[1,1,128]{2,1,0:T(2,128)(2,1)} %bitcast.472), channel_id=1, replica_groups=mesh['group'=4,'blk'=4,'head'=2] {'blk','head'}, dimensions={0}, use_global_device_ids=true | all-gather | bytes 2304 | tf_op jit(solution)/shard_map/all_gather | solution.py:78
  31.9 17.2 %all-gather.15.cloned.1.call-done = bf16[1024,512]{1,0:T(8,128)(2,1)} async-done(((bf16[128,512]{1,0:T(8,128)(2,1)}), bf16[1024,512]{1,0:T(8,128)(2,1)}) %all-gather.15.cloned.1.call-update) | async-done | bytes 1048592 | tf_op jit(solution)/shard_map/all_gather | solution.py:75
  51.6 3.4 all-to-all-start.2
  55.2 7.6 all-to-all-done.2
  64.4 21.3 %all-gather.9.cloned.1.call-done = bf16[1024,512]{1,0:T(8,128)(2,1)} async-done(((bf16[128,512]{1,0:T(8,128)(2,1)}), bf16[1024,512]{1,0:T(8,128)(2,1)}) %all-gather.9.cloned.1.call-update) | async-done | bytes 1048592 | tf_op jit(solution)/shard_map/all_gather | solution.py:74
  88.1 7.8 all_to_all.198
  98.2 18.0 %reduce-window.6 = s32[2,32,8,128]{3,2,1,0:T(8,128)S(1)} reduce-window(s32[2,32,8,128]{3,2,1,0:T(8,128)S(1)} %fusion.84, s32[]{:T(128)} %constant.56.clone.1), window={size=1x1x1x128 pad=0_0x0_0x0_0x127_0}, to_apply=%region_8.9 | reduce-window | flops 8323072 | bytes 524292 | tf_op jit(solution)/shard_map/reduce-window
  117.6 20.1 %all-gather.13.cloned.1.call-done = bf16[1024,1024]{1,0:T(8,128)(2,1)} async-done(((bf16[128,1024]{1,0:T(8,128)(2,1)}), bf16[1024,1024]{1,0:T(8,128)(2,1)}) %all-gather.13.cloned.1.call-update) | async-done | bytes 2097168 | tf_op jit(solution)/shard_map/all_gather | solution.py:73
  137.7 2.9 copy.122
  142.9 3.5 all-to-all-start.1
  147.5 6.9 all-to-all-done.1
  155.3 9.8 all-gather.17.cloned.1.call-done
  165.1 28.8 %all-gather.11.cloned.1.call-done = bf16[2,1024,256]{1,2,0:T(8,128)(2,1)} async-done(((bf16[2,256,256]{1,2,0:T(8,128)(2,1)}), bf16[2,1024,256]{1,2,0:T(8,128)(2,1)}) %all-gather.11.cloned.1.call-update) | async-done | bytes 1048592 | tf_op jit(solution)/shard_map/all_gather | solution.py:147
  193.9 17.8 %while.30 = (s32[]{:T(128)}, f32[2,256,4,2]{1,3,2,0:T(2,128)S(1)}, f32[2,256,4,2]{1,3,2,0:T(2,128)S(1)}, f32[2,256,4,2,64]{1,4,3,2,0:T(8,128)S(1)}, s32[2]{0:T(1...) while((s32[]{:T(128)}, f32[2,256,4,2]{1,3,2,0:T(2,128)S(1)}, ...), condition=%wide.region_4.5_spmd.clone, body=%wide.region_1.4_spmd.clone.sunk | while | flops 565596928 | bytes 32526568 | solution.py:173
  213.0 3.7 all-to-all-start.3
  216.7 24.5 %all-gather.1 = bf16[8,1,128]{2,1,0:T(2,128)(2,1)S(1)} all-gather(bf16[1,1,128]{2,1,0:T(2,128)(2,1)S(1)} %bitcast.473), channel_id=1, replica_groups=mesh['group'=4,'blk'=4,'head'=2] {'blk','head'}, dimensions={0}, use_global_device_ids=true | all-gather | bytes 2304 | tf_op jit(solution)/shard_map/all_gather | solution.py:79
  242.2 8.0 all-gather.19.cloned.1.call-done
  252.8 12.7 scatter_custom_fusion
  265.6 59.5 %all_to_all.199 = bf16[32,72,1024]{2,1,0:T(8,128)(2,1)S(1)} all-to-all(bf16[32,72,1024]{2,1,0:T(8,128)(2,1)} %bitcast.402), channel_id=1, replica_groups=mesh['group'=4,'blk'=4,'head'=2] {'blk','head'}, dimensions={0} | all-to-all | bytes 9437184 | tf_op jit(solution)/shard_map/all_to_all | solution.py:204
  325.8 2.8 copy-done.9
  331.3 4.6 multiply_convert_fusion.2
  339.4 5.8 copy.137
  345.2 4.8 all-to-all-start.5
  350.1 77.9 %all_gather.35 = bf16[1024,32]{0,1:T(8,128)(2,1)S(1)} all-gather(bf16[128,32]{0,1:T(8,128)(2,1)S(1)} %copy-done.44), channel_id=1, replica_groups=mesh['group'=4,'blk'=4,'head'=2] {'blk','head'}, dimensions={0}, use_global_device_ids=true | all-gather | bytes 73728 | tf_op jit(solution)/shard_map/all_gather | solution.py:77
  430.8 6.2 copy.138
  437.1 42.1 %gather_fusion = bf16[2048,1024]{1,0:T(8,128)(2,1)} fusion(bf16[32,72,1024]{2,1,0:T(8,128)(2,1)} %bitcast.389, s32[2048]{0:T(1024)S(1)} %bitcast.387), kind=kCustom, calls=%fused_computation | custom fusion | bytes 8404992 | tf_op jit(solution)/shard_map/gather | solution.py:212
  479.2 4.5 fusion.49
  484.6 13.5 scatter_custom_fusion.1
  498.1 53.4 %all_to_all.200 = bf16[32,72,1024]{2,1,0:T(8,128)(2,1)S(1)} all-to-all(bf16[32,72,1024]{2,1,0:T(8,128)(2,1)} %bitcast.399), channel_id=1, replica_groups=mesh['group'=4,'blk'=4,'head'=2] {'blk','head'}, dimensions={0} | all-to-all | bytes 9437184 | tf_op jit(solution)/shard_map/all_to_all | solution.py:229
  552.0 3.3 copy-done.52
  555.4 7.9 multiply_convert_fusion
  563.3 5.2 fusion.94
  568.5 7.7 add_convert_fusion
  576.2 8.2 copy.140
  584.4 5.2 all-to-all-start.7
  590.2 3.5 fusion.51
  593.7 44.5 %all-to-all-done.7 = bf16[4,576,1024]{2,0,1:T(4,128)(2,1)} async-done(((bf16[4,576,1024]{2,0,1:T(4,128)(2,1)}), bf16[4,576,1024]{2,0,1:T(4,128)(2,1)}, u32[]{:S(2)}, u32[]{:S(2)}) %all-to-all-start.7) | async-done | bytes 4718624 | tf_op jit(solution)/shard_map/all_to_all | solution.py:253
  638.2 6.2 copy.141
  644.5 42.0 %gather_fusion.1 = bf16[2048,1024]{1,0:T(8,128)(2,1)} fusion(bf16[32,72,1024]{2,1,0:T(8,128)(2,1)} %bitcast.390, s32[2048]{0:T(1024)S(1)} %bitcast.388), kind=kCustom, calls=%fused_computation.1 | custom fusion | bytes 8404992 | tf_op jit(solution)/shard_map/gather | solution.py:257
  686.5 5.5 convert_reduce_fusion
  696.6 4.9 all-to-all-start.8
  701.7 8.7 all-to-all-done.8
  713.2 25.4 %while.31 = (s32[]{:T(128)}, f32[2,256,4,2,64]{1,4,3,2,0:T(8,128)}, f32[2,1024,4,64]{1,3,2,0:T(8,128)S(1)}, f32[2,1024,4,64]{1,3,2,0:T(8,128)}, s32[2]{0:T(128)S...) while((s32[]{:T(128)}, f32[2,256,4,2,64]{1,4,3,2,0:T(8,128)}, ...), condition=%wide.region_18.19_spmd.clone, body=%wide.region_17.18_spmd.clone.sunk | while | flops 1371144960 | bytes 76091760 | solution.py:319
  720.4 3.2 fusion.200
  733.0 3.2 fusion.200
  742.7 3.3 convolution_convert_fusion.4
  746.1 22.3 %reduce-scatter.12.cloned.1.call-done = bf16[2,256,256]{1,2,0:T(8,128)(2,1)} async-done(((bf16[2,1024,256]{1,2,0:T(8,128)(2,1)}), bf16[2,256,256]{1,2,0:T(8,128)(2,1)}) %reduce-scatter.12.cloned.1.call-update) | async-done | bytes 262160 | tf_op jit(solution)/shard_map/reduce_scatter | solution.py:332
  769.5 7.8 all_to_all.201
  780.1 19.7 %reduce-scatter.10.cloned.1.call-done = bf16[2,256,256]{1,2,0:T(8,128)(2,1)} async-done(((bf16[2,1024,256]{1,2,0:T(8,128)(2,1)}), bf16[2,256,256]{1,2,0:T(8,128)(2,1)}) %reduce-scatter.10.cloned.1.call-update) | async-done | bytes 262160 | tf_op jit(solution)/shard_map/reduce_scatter | solution.py:324
  801.2 7.8 all_to_all.202
  811.7 17.2 %all_to_all.203 = bf16[2,256,512]{2,0,1:T(2,128)(2,1)S(1)} all-to-all(bf16[2,256,512]{2,0,1:T(2,128)(2,1)S(1)} %copy.144), channel_id=1, replica_groups=mesh['group'=4,'blk'=4,'head'=2] {'head'}, dimensions={1} | all-to-all | bytes 1048576 | tf_op jit(solution)/shard_map/all_to_all | solution.py:361
  833.0 8.7 convolution_convert_fusion.1
  841.8 8.3 convolution_convert_fusion.2
  850.1 8.2 convolution_convert_fusion.3
  858.3 37.3 %reduce-scatter.18.cloned.1.call-done = bf16[128,512]{1,0:T(8,128)(2,1)} async-done(((bf16[1024,512]{1,0:T(8,128)(2,1)}), bf16[128,512]{1,0:T(8,128)(2,1)}) %reduce-scatter.18.cloned.1.call-update) | async-done | bytes 131088 | tf_op jit(solution)/shard_map/reduce_scatter | solution.py:393
  895.6 38.3 %reduce-scatter.16.cloned.1.call-done = bf16[128,512]{1,0:T(8,128)(2,1)} async-done(((bf16[1024,512]{1,0:T(8,128)(2,1)}), bf16[128,512]{1,0:T(8,128)(2,1)}) %reduce-scatter.16.cloned.1.call-update) | async-done | bytes 131088 | tf_op jit(solution)/shard_map/reduce_scatter | solution.py:390
  933.9 50.3 %reduce-scatter.14.cloned.1.call-done = bf16[128,1024]{1,0:T(8,128)(2,1)} async-done(((bf16[1024,1024]{1,0:T(8,128)(2,1)}), bf16[128,1024]{1,0:T(8,128)(2,1)}) %reduce-scatter.14.cloned.1.call-update) | async-done | bytes 262160 | tf_op jit(solution)/shard_map/reduce_scatter | solution.py:387
  986.1 33.2 %reduce-scatter.22.cloned.1.call-done = bf16[128,32]{1,0:T(8,128)(2,1)} async-done(((bf16[1024,32]{1,0:T(8,128)(2,1)}), bf16[128,32]{1,0:T(8,128)(2,1)}) %reduce-scatter.22.cloned.1.call-update) | async-done | bytes 8208
  1025.1 16.1 %all-reduce.2 = (bf16[1024]{0:T(1024)(128)(2,1)S(1)}, bf16[1024]{0:T(1024)(128)(2,1)S(1)}) all-reduce(bf16[1024]{0:T(1024)(128)(2,1)S(1)} %get-tuple-element.240, bf16[1024]{0:T(1024)(128)(2,1)S(1)} %get-tuple-element.238), channel_id=4, replica_groups=mesh['group'=4,'blk'=4,'head'=2] {'blk','head'}, use_global_device_ids=true, to_apply=%region_23.24.clone | all-reduce | flops 2048 | bytes 8192
  1041.3 10.7 all-reduce.3
  1055.0 421.0 %all-reduce.7.cloned.1.call-done = (bf16[128,1024]{1,0:T(8,128)(2,1)}, bf16[128,512]{1,0:T(8,128)(2,1)}, bf16[128,512]{1,0:T(8,128)(2,1)}, bf16[128,1024]{1,0:T(...) async-done(((bf16[128,1024]{1,0:T(8,128)(2,1)}, bf16[128,512]{1,0:T(8,128)(2,1)}, ...) | async-done | bytes 13369360 | tf_op jit(solution)/shard_map/psum | solution.py:410
  1482.9 6.9 convert_element_type.276
  1489.8 4.6 convert_element_type.278
  1494.4 4.4 convert_element_type.280
  (326 shorter events, 110.1 us)
Async XLA Ops:
  7.2 57.0 %copy-start.5 = (bf16[2,128,1024]{2,1,0:T(8,128)(2,1)S(1)}, bf16[2,128,1024]{2,1,0:T(8,128)(2,1)}, u32[]{:S(2)}) copy-start(bf16[2,128,1024]{2,1,0:T(8,128)(2,1)} %param.18) | copy-start | bytes 1572868
  7.2 41.9 %all-gather.15.cloned.1.call-start = ((), (), s32[]{:S(2)}) async-start(), calls=%async_computation.22 | async-start | bytes 1179648 | tf_op jit(solution)/shard_map/all_gather | solution.py:75
  7.9 77.8 %all-gather.9.cloned.1.call-start = ((), (), s32[]{:S(2)}) async-start(), calls=%async_computation.19 | async-start | bytes 1179648 | tf_op jit(solution)/shard_map/all_gather | solution.py:74
  8.7 129.0 %all-gather.13.cloned.1.call-start = ((), (), s32[]{:S(2)}) async-start(), calls=%async_computation.21 | async-start | bytes 2359296 | tf_op jit(solution)/shard_map/all_gather | solution.py:73
  28.9 58.8 %copy-start.37 = (f32[8,1,128]{2,1,0:T(1,128)}, f32[8,1,128]{2,1,0:T(1,128)S(1)}, u32[]{:S(2)}) copy-start(f32[8,1,128]{2,1,0:T(1,128)S(1)} %convert_element_type.283) | copy-start | bytes 12292
  30.1 57.6 %copy-start.40 = (f32[2,128]{1,0:T(2,128)}, f32[2,128]{1,0:T(2,128)S(1)}, u32[]{:S(2)}) copy-start(f32[2,128]{1,0:T(2,128)S(1)} %fusion.67) | copy-start | bytes 3076
  51.6 11.2 all-to-all-start.2
  55.1 110.0 %all-gather.17.cloned.1.call-start = ((), (), s32[]{:S(2)}) async-start(), calls=%async_computation.23 | async-start | bytes 1310720 | tf_op jit(solution)/shard_map/all_gather | solution.py:148
  55.1 30.6 %copy-start.46 = (f32[32]{0:T(128)}, f32[32]{0:T(128)S(1)}, u32[]{:S(2)}) copy-start(f32[32]{0:T(128)S(1)} %multiply_power_fusion) | copy-start | bytes 388
  64.0 129.9 %all-gather.11.cloned.1.call-start = ((), (), s32[]{:S(2)}) async-start(), calls=%async_computation.20 | async-start | bytes 1310720 | tf_op jit(solution)/shard_map/all_gather | solution.py:147
  64.4 76.2 %copy-start.3 = (bf16[2,128,1024]{2,1,0:T(8,128)(2,1)}, bf16[2,128,1024]{2,1,0:T(8,128)(2,1)S(1)}, u32[]{:S(2)}) copy-start(bf16[2,128,1024]{2,1,0:T(8,128)(2,1)S(1)} %fusion.69) | copy-start | bytes 1572868
  64.4 33.3 %copy-start.39 = (s32[2,128,8]{1,2,0:T(8,128)S(1)}, s32[2,128,8]{1,2,0:T(8,128)}, u32[]{:S(2)}) copy-start(s32[2,128,8]{1,2,0:T(8,128)} %param.20) | copy-start | bytes 24580
  97.1 153.1 %all-gather.19.cloned.1.call-start = ((), (), s32[]{:S(2)}) async-start(), calls=%async_computation.24 | async-start | bytes 2359296 | tf_op jit(solution)/shard_map/all_gather | solution.py:76
  140.6 7.0 copy-start.34
  141.3 52.5 %copy-start.24 = (f32[2,256,4,2,64]{1,4,3,2,0:T(8,128)S(1)}, f32[2,256,4,2,64]{1,4,3,2,0:T(8,128)}, u32[]{:S(2)}) copy-start(f32[2,256,4,2,64]{1,4,3,2,0:T(8,128)} %custom-call.6) | copy-start | bytes 3145732
  142.9 11.5 all-to-all-start.1
  193.9 22.9 %copy-start.48 = (bf16[128]{0:T(256)(128)(2,1)S(1)}, bf16[128]{0:T(256)(128)(2,1)}, u32[]{:S(2)}) copy-start(bf16[128]{0:T(256)(128)(2,1)} %param.23) | copy-start | bytes 772
  193.9 47.4 %copy-start.50 = (s32[2]{0:T(128)S(1)}, s32[2]{0:T(128)}, u32[]{:S(2)}) copy-start(s32[2]{0:T(128)} %constant.110) | copy-start | bytes 28
  193.9 47.5 %copy-start.49 = (s32[2]{0:T(128)S(1)}, s32[2]{0:T(128)}, u32[]{:S(2)}) copy-start(s32[2]{0:T(128)} %constant.113) | copy-start | bytes 28
  211.7 38.6 %copy-start.25 = (f32[2,256,4,2,64]{1,4,3,2,0:T(8,128)}, f32[2,256,4,2,64]{1,4,3,2,0:T(8,128)S(1)}, u32[]{:S(2)}) copy-start(f32[2,256,4,2,64]{1,4,3,2,0:T(8,128)S(1)} %get-tuple-element.145) | copy-start | bytes 3145732
  213.0 28.5 %all-to-all-start.3 = ((bf16[2,256,512]{2,0,1:T(2,128)(2,1)}), bf16[2,256,512]{2,0,1:T(2,128)(2,1)S(1)}, u32[]{:S(2)}, u32[]{:S(2)}) async-start(bf16[2,256,512]{2,0,1:T(2,128)(2,1)} %copy.127), calls=%async_computation.3 | async-start | bytes 1048576 | tf_op jit(solution)/shard_map/all_to_all | solution.py:182
  242.2 23.4 %copy-start.16 = (bf16[32,8,2,512]{3,1,2,0:T(8,128)(2,1)}, bf16[32,8,2,512]{3,1,2,0:T(8,128)(2,1)S(1)}, u32[]{:S(2)}) copy-start(bf16[32,8,2,512]{3,1,2,0:T(8,128)(2,1)S(1)} %copy.174) | copy-start | bytes 1572868
  252.8 176.3 %copy-start.13 = (bf16[256,1024]{1,0:T(8,128)(2,1)}, bf16[256,1024]{1,0:T(8,128)(2,1)S(1)}, u32[]{:S(2)}) copy-start(bf16[256,1024]{1,0:T(8,128)(2,1)S(1)} %multiply_convert_fusion.3) | copy-start | bytes 1572868
  325.1 3.5 copy-start.9
  325.8 5.4 copy-start.18
  331.2 4.6 copy-start.54
  331.2 5.3 copy-start.51
  345.2 4.9 copy-start.44
  345.2 85.7 %all-to-all-start.5 = ((bf16[4,576,1024]{2,0,1:T(4,128)(2,1)}), bf16[4,576,1024]{2,0,1:T(4,128)(2,1)}, u32[]{:S(2)}, u32[]{:S(2)}) async-start(bf16[4,576,1024]{2,0,1:T(4,128)(2,1)} %copy.137), calls=%async_computation.5 | async-start | bytes 9437184 | tf_op jit(solution)/shard_map/all_to_all | solution.py:211
  350.1 87.0 %copy-start.35 = (s32[256,8]{1,0:T(8,128)}, s32[256,8]{1,0:T(8,128)S(1)}, u32[]{:S(2)}) copy-start(s32[256,8]{1,0:T(8,128)S(1)} %copy.130) | copy-start | bytes 24580
  437.1 42.1 %copy-start.29 = (bf16[2,128,1024]{2,1,0:T(8,128)(2,1)S(1)}, bf16[2,128,1024]{2,1,0:T(8,128)(2,1)}, u32[]{:S(2)}) copy-start(bf16[2,128,1024]{2,1,0:T(8,128)(2,1)} %param.21) | copy-start | bytes 1572868
  479.2 4.5 copy-start.45
  551.5 3.9 copy-start.52
  552.0 11.3 copy-start.19
  584.4 5.2 copy-start.31
  584.4 5.3 copy-start.36
  584.4 53.8 %all-to-all-start.7 = ((bf16[4,576,1024]{2,0,1:T(4,128)(2,1)}), bf16[4,576,1024]{2,0,1:T(4,128)(2,1)}, u32[]{:S(2)}, u32[]{:S(2)}) async-start(bf16[4,576,1024]{2,0,1:T(4,128)(2,1)} %copy.140), calls=%async_computation.7 | async-start | bytes 9437184 | tf_op jit(solution)/shard_map/all_to_all | solution.py:253
  590.2 101.8 %copy-start.32 = (f32[256,1,32]{2,1,0:T(1,128)}, f32[256,1,32]{2,1,0:T(1,128)S(1)}, u32[]{:S(2)}) copy-start(f32[256,1,32]{2,1,0:T(1,128)S(1)} %fusion.72) | copy-start | bytes 98308
  693.7 17.5 %copy-start.26 = (f32[2,256,4,2,64]{1,4,3,2,0:T(8,128)S(1)}, f32[2,256,4,2,64]{1,4,3,2,0:T(8,128)}, u32[]{:S(2)}) copy-start(f32[2,256,4,2,64]{1,4,3,2,0:T(8,128)} %copy-done.25) | copy-start | bytes 3145732
  696.6 13.7 all-to-all-start.8
  701.5 66.9 %reduce-scatter.12.cloned.1.call-start = ((), (), s32[]{:S(2)}) async-start(), calls=%async_computation.26 | async-start | bytes 1310720 | tf_op jit(solution)/shard_map/reduce_scatter | solution.py:332
  738.6 4.1 copy-start.17
  741.4 58.5 %reduce-scatter.10.cloned.1.call-start = ((), (), s32[]{:S(2)}) async-start(), calls=%async_computation.25 | async-start | bytes 1310720 | tf_op jit(solution)/shard_map/reduce_scatter | solution.py:324
  742.6 35.8 %copy-start.4 = (bf16[2,128,1024]{2,1,0:T(8,128)(2,1)S(1)}, bf16[2,128,1024]{2,1,0:T(8,128)(2,1)}, u32[]{:S(2)}) copy-start(bf16[2,128,1024]{2,1,0:T(8,128)(2,1)} %copy-done.3) | copy-start | bytes 1572868
  742.6 115.6 %reduce-scatter.20.cloned.1.call-start = ((), (), s32[]{:S(2)}) async-start(), calls=%async_computation.30 | async-start | bytes 2359296 | tf_op jit(solution)/shard_map/reduce_scatter | solution.py:396
  746.0 33.9 %copy-start.47 = (f32[32]{0:T(128)S(1)}, f32[32]{0:T(128)}, u32[]{:S(2)}) copy-start(f32[32]{0:T(128)} %copy-done.46) | copy-start | bytes 388
  746.0 149.5 %reduce-scatter.18.cloned.1.call-start = ((), (), s32[]{:S(2)}) async-start(), calls=%async_computation.29 | async-start | bytes 1179648 | tf_op jit(solution)/shard_map/reduce_scatter | solution.py:393
  779.8 31.1 %copy-start.2 = (f32[2,256,4,2,64]{1,4,3,2,0:T(8,128)S(1)}, f32[2,256,4,2,64]{1,4,3,2,0:T(8,128)}, u32[]{:S(2)}) copy-start(f32[2,256,4,2,64]{1,4,3,2,0:T(8,128)} %get-tuple-element.148) | copy-start | bytes 3145732
  779.9 154.0 %reduce-scatter.16.cloned.1.call-start = ((), (), s32[]{:S(2)}) async-start(), calls=%async_computation.28 | async-start | bytes 1179648 | tf_op jit(solution)/shard_map/reduce_scatter | solution.py:390
  810.9 173.3 %reduce-scatter.14.cloned.1.call-start = ((), (), s32[]{:S(2)}) async-start(), calls=%async_computation.27 | async-start | bytes 2359296 | tf_op jit(solution)/shard_map/reduce_scatter | solution.py:387
  811.7 20.2 %copy-start.14 = (bf16[256,1024]{1,0:T(8,128)(2,1)S(1)}, bf16[256,1024]{1,0:T(8,128)(2,1)}, u32[]{:S(2)}) copy-start(bf16[256,1024]{1,0:T(8,128)(2,1)} %copy-done.13) | copy-start | bytes 1572868
  811.7 20.2 %copy-start.33 = (f32[256,1,32]{2,1,0:T(1,128)S(1)}, f32[256,1,32]{2,1,0:T(1,128)}, u32[]{:S(2)}) copy-start(f32[256,1,32]{2,1,0:T(1,128)} %copy-done.32) | copy-start | bytes 98308
  831.8 187.5 %reduce-scatter.22.cloned.1.call-start = ((), (), s32[]{:S(2)}) async-start(), calls=%async_computation.31 | async-start | bytes 294912
  833.0 643.1 %all-reduce.7.cloned.1.call-start = ((), (), s32[]{:S(2)}) async-start(), calls=%async_computation.32 | async-start | bytes 26738688 | tf_op jit(solution)/shard_map/psum | solution.py:410
  833.0 8.7 copy-start.27
  841.8 8.3 copy-start.15
  984.2 38.3 %copy-start.23 = (bf16[1024,512]{1,0:T(8,128)(2,1)S(1)}, bf16[1024,512]{1,0:T(8,128)(2,1)}, u32[]{:S(2)}) copy-start(bf16[1024,512]{1,0:T(8,128)(2,1)} %all-gather.9.cloned.1.call-done) | copy-start | bytes 3145732
  984.3 38.8 %copy-start.6 = (bf16[2,128,1024]{2,1,0:T(8,128)(2,1)S(1)}, bf16[2,128,1024]{2,1,0:T(8,128)(2,1)}, u32[]{:S(2)}) copy-start(bf16[2,128,1024]{2,1,0:T(8,128)(2,1)} %param.18) | copy-start | bytes 1572868
  984.3 38.8 %copy-start.38 = (f32[8,1,128]{2,1,0:T(1,128)S(1)}, f32[8,1,128]{2,1,0:T(1,128)}, u32[]{:S(2)}) copy-start(f32[8,1,128]{2,1,0:T(1,128)} %copy-done.37) | copy-start | bytes 12292
  984.3 38.8 %copy-start.43 = (f32[256]{0:T(256)S(1)}, f32[256]{0:T(256)}, u32[]{:S(2)}) copy-start(f32[256]{0:T(256)} %copy-done.42) | copy-start | bytes 3076
  1020.1 33.6 %copy-start.41 = (f32[2,128]{1,0:T(2,128)S(1)}, f32[2,128]{1,0:T(2,128)}, u32[]{:S(2)}) copy-start(f32[2,128]{1,0:T(2,128)} %copy-done.40) | copy-start | bytes 3076
  1020.1 33.6 %copy-start.8 = (f32[256,1024]{1,0:T(8,128)S(1)}, f32[256,1024]{1,0:T(8,128)}, u32[]{:S(2)}) copy-start(f32[256,1024]{1,0:T(8,128)} %copy-done.7) | copy-start | bytes 3145732
  1482.9 6.9 copy-start.22
  1489.8 4.6 copy-start.21
  (16 other events, 31.5 us)
Sparse Core Ops, SparseCore 0:
  9.6 39.4 all-gather.14
  50.6 35.0 all-gather.8
  87.2 50.3 all-gather.12
  139.9 25.1 all-gather.16
  167.3 26.4 all-gather.10
  195.2 54.9 all-gather.18
  741.5 26.7 reduce-scatter.11
  772.1 27.7 reduce-scatter.9
  802.2 55.1 reduce-scatter.19
  859.5 35.9 reduce-scatter.17
  897.9 35.9 reduce-scatter.15
  936.0 48.1 reduce-scatter.13
  987.0 32.1 reduce-scatter.21
  1023.6 452.4 all-reduce.6
where the time goes:
time: 1520 us; the launch traced here: 1510 us
  waiting for transfers between devices  798 us (52%)
  blocking collectives  302 us (20%)
  local copies, waits for them, and re-layouts  166 us (11%)
  matrix products  112 us (7%)
  other arithmetic  82.6 us (5%)
  starting transfers between devices  26.2 us (2%)
  between operations  16.2 us (1%)
    psum x1, waiting for transfers between devices, on_device(): lax.psum(query_shard.astype(jnp.bfloat16), 'group').astype(jnp.float32)  421 us
    all_gather x1, blocking collectives, on_device(): lax.all_gather(router_weight, ('blk', 'head'), axis=0, tiled=True)  77.9 us
    all_to_all x1, blocking collectives, on_device(): lax.all_to_all(outgoing, ('blk', 'head'), split_axis=0, concat_axis=1, ti...  59.5 us
    all_to_all x1, blocking collectives, on_device(): lax.all_to_all(grad_outgoing, ('blk', 'head'), split_axis=0, concat_axis=...  53.4 us
    reduce_scatter x1, waiting for transfers between devices, on_device(): lax.psum_scatter(query_weight_grad.astype(jnp.bfloat16), ('blk', 'head'),...  50.3 us
    all_to_all x1, waiting for transfers between devices, on_device(): lax.all_to_all(pair_back, ('blk', 'head'), split_axis=1, concat_axis=0, t...  44.5 us
    gather x1, local copies, waits for them, and re-layouts, on_device(): returned[targets, slot_index].reshape(number_of_tokens, TOP, width_dim)  42.1 us
    gather x1, local copies, waits for them, and re-layouts, on_device(): grad_returned[targets, slot_index].reshape(number_of_tokens, TOP, width_dim)  42 us
  transfers between devices with their start and end apart: 20, of which 17 were waited for; matrix products, arithmetic and copies ran while one was open for 7% of the time, Pallas kernels for 0%

commit v1 on v0

--- a/solution.py
+++ b/solution.py
@@ -1,6 +1,10 @@
+import functools
+
 import jax
 import jax.numpy as jnp
 from jax import lax
+from jax.experimental import pallas as pl
+from jax.experimental.pallas import tpu as pltpu
 from jax.sharding import PartitionSpec as P
 
 QUERY_HEADS = 16
@@ -434,6 +438,1074 @@
     )
 
 
+bf16 = jnp.bfloat16
+f32 = jnp.float32
+MESH_ID = pl.DeviceIdType.MESH
+VMEM_LIMIT = 66 * 1000 * 1000
+COLOURS = ((0, 96), (96, 80), (176, 80))
+LINKS = (("head", 1), ("blk", 1), ("blk", 2), ("group", 2), ("group", 1))
+ORDERS = ((0, 1, 2), (1, 2, 0), (2, 0, 1))
+
+
+def vmem():
+    return pl.BlockSpec(memory_space=pltpu.VMEM)
+
+
+def anywhere():
+    return pl.BlockSpec(memory_space=pl.ANY)
+
+
+def swap(value, link):
+    axis, step = LINKS[link]
+    count = lax.axis_size(axis)
+    return lax.ppermute(value, axis, [(i, i ^ step) for i in range(count)])
+
+
+def gather_swaps(value, order):
+    held = value[None]
+    for link in order:
+        held = jnp.concatenate([held, swap(held, link)], 0)
+    return held
+
+
+def gather_rows(rows):
+    return tuple(
+        gather_swaps(rows[start : start + count], ORDERS[k])
+        for k, (start, count) in enumerate(COLOURS)
+    )
+
+
+def dot_last(left, right):
+    return lax.dot_general(left, right, (((1,), (1,)), ((), ())), preferred_element_type=f32)
+
+
+def dot_first(left, right):
+    return lax.dot_general(left, right, (((0,), (0,)), ((), ())), preferred_element_type=f32)
+
+
+def dot(left, right):
+    return jnp.dot(left, right, preferred_element_type=f32)
+
+
+def my_place():
+    return lax.axis_index("blk") * 2 + lax.axis_index("head")
+
+
+def peer(step):
+    place = lax.rem(my_place() + step, 8)
+    return place, {"blk": place // 2, "head": lax.rem(place, 2)}
+
+
+def neighbour(link):
+    if link == 0:
+        return {"head": 1 - lax.axis_index("head")}
+    blk = lax.axis_index("blk")
+    if link == 1:
+        return {"blk": blk + 1 - 2 * lax.rem(blk, 2)}
+    return {"blk": lax.rem(blk + 2, 4)}
+
+
+def my_bits():
+    blk = lax.axis_index("blk")
+    return (lax.axis_index("head"), lax.rem(blk, 2), blk // 2)
+
+
+def meet_all():
+    barrier = pltpu.get_barrier_semaphore()
+    for step in range(1, 8):
+        pl.semaphore_signal(barrier, 1, device_id=peer(step)[1], device_id_type=MESH_ID)
+    pl.semaphore_wait(barrier, 7)
+
+
+def remote(src, dst, send, recv, target):
+    return pltpu.make_async_remote_copy(
+        src_ref=src, dst_ref=dst, send_sem=send, recv_sem=recv, device_id=target, device_id_type=MESH_ID
+    )
+
+
+def cube_index(bits, fixed, rows):
+    entries = [pl.ds(fixed[link], 1) if link in fixed else pl.ds(0, 2) for link in (2, 1, 0)]
+    return tuple(entries) + (pl.ds(*rows),)
+
+
+def cube_gather(src, dst, send, recv, local_sem):
+    bits = my_bits()
+    own = pltpu.make_async_copy(src, dst.at[bits[2], bits[1], bits[0]], local_sem)
+    own.start()
+    started = []
+    for step in range(3):
+        now = []
+        for k, order in enumerate(ORDERS):
+            fixed = {link: bits[link] for link in order[step:]}
+            where = dst.at[cube_index(bits, fixed, COLOURS[k])]
+            if step == 0:
+                start, count = COLOURS[k]
+                here = src.at[pl.ds(start, count)]
+                where = dst.at[bits[2], bits[1], bits[0], pl.ds(start, count)]
+            else:
+                here = where
+            copy = remote(here, where, send.at[step, k], recv.at[step, k], neighbour(order[step]))
+            copy.start()
+            now.append(copy)
+        if step == 0:
+            own.wait()
+        for copy in now:
+            copy.wait_recv()
+        started += now
+    return started
+
+
+def front_kernel(
+    tok, wq, wkv, gains, router, routes, tok_all, w_all, gains_all, router_all, routes_all,
+    send, recv, small_send, small_recv, local_sem, own_sem,
+):
+    me = my_place()
+    meet_all()
+    smalls = []
+    for step in range(1, 8):
+        place, target = peer(step)
+        pairs = (
+            (wq.at[:, pl.ds(place * 128, 128)], w_all.at[pl.ds(me * 128, 128), pl.ds(0, 128)]),
+            (wkv.at[:, pl.ds(place * 128, 128)], w_all.at[pl.ds(me * 128, 128), pl.ds(128, 128)]),
+            (gains, gains_all.at[:, pl.ds(me * 128, 128)]),
+            (router, router_all.at[pl.ds(me * 128, 128)]),
+            (routes, routes_all.at[:, pl.ds(me * 256, 256)]),
+        )
+        for kind, (src, dst) in enumerate(pairs):
+            copy = remote(src, dst, small_send.at[kind, step], small_recv.at[kind, step], target)
+            copy.start()
+            smalls.append(copy)
+    own = (
+        (wq.at[:, pl.ds(me * 128, 128)], w_all.at[pl.ds(me * 128, 128), pl.ds(0, 128)]),
+        (wkv.at[:, pl.ds(me * 128, 128)], w_all.at[pl.ds(me * 128, 128), pl.ds(128, 128)]),
+        (gains, gains_all.at[:, pl.ds(me * 128, 128)]),
+        (router, router_all.at[pl.ds(me * 128, 128)]),
+        (routes, routes_all.at[:, pl.ds(me * 256, 256)]),
+    )
+    locals_ = []
+    for kind, (src, dst) in enumerate(own):
+        copy = pltpu.make_async_copy(src, dst, own_sem.at[kind])
+        copy.start()
+        locals_.append(copy)
+    started = cube_gather(tok, tok_all, send, recv, local_sem)
+    for copy in locals_:
+        copy.wait()
+    for copy in smalls:
+        copy.wait()
+    for copy in started:
+        copy.wait_send()
+
+
+def front(tok, wq, wkv, gains, router, routes):
+    width = tok.shape[1]
+    return pl.pallas_call(
+        front_kernel,
+        out_shape=(
+            jax.ShapeDtypeStruct((2, 2, 2, 256, width), bf16),
+            jax.ShapeDtypeStruct((width, 256), bf16),
+            jax.ShapeDtypeStruct((16, width), bf16),
+            jax.ShapeDtypeStruct((width, 32), bf16),
+            jax.ShapeDtypeStruct((8, 2048), jnp.int32),
+        ),
+        in_specs=[vmem()] * 6,
+        out_specs=(vmem(),) * 5,
+        scratch_shapes=[
+            pltpu.SemaphoreType.DMA((3, 3)),
+            pltpu.SemaphoreType.DMA((3, 3)),
+            pltpu.SemaphoreType.DMA((5, 8)),
+            pltpu.SemaphoreType.DMA((5, 8)),
+            pltpu.SemaphoreType.DMA,
+            pltpu.SemaphoreType.DMA((5,)),
+        ],
+        compiler_params=pltpu.CompilerParams(
+            collective_id=0, has_side_effects=True, vmem_limit_bytes=VMEM_LIMIT
+        ),
+        name="front",
+    )(tok, wq, wkv, gains, router, routes)
+
+
+def rows_gather_kernel(rows, small, rows_all, small_all, send, recv, small_send, small_recv, local_sem, own_sem):
+    me = my_place()
+    meet_all()
+    smalls = []
+    for step in range(1, 8):
+        copy = remote(
+            small, small_all.at[:, pl.ds(me * 256, 256)], small_send.at[step], small_recv.at[step], peer(step)[1]
+        )
+        copy.start()
+        smalls.append(copy)
+    own = pltpu.make_async_copy(small, small_all.at[:, pl.ds(me * 256, 256)], own_sem)
+    own.start()
+    started = cube_gather(rows, rows_all, send, recv, local_sem)
+    own.wait()
+    for copy in smalls:
+        copy.wait()
+    for copy in started:
+        copy.wait_send()
+
+
+def rows_gather(rows, small):
+    return pl.pallas_call(
+        rows_gather_kernel,
+        out_shape=(
+            jax.ShapeDtypeStruct((2, 2, 2) + rows.shape, bf16),
+            jax.ShapeDtypeStruct((8, 2048), f32),
+        ),
+        in_specs=[vmem()] * 2,
+        out_specs=(vmem(),) * 2,
+        scratch_shapes=[
+            pltpu.SemaphoreType.DMA((3, 3)),
+            pltpu.SemaphoreType.DMA((3, 3)),
+            pltpu.SemaphoreType.DMA((8,)),
+            pltpu.SemaphoreType.DMA((8,)),
+            pltpu.SemaphoreType.DMA,
+            pltpu.SemaphoreType.DMA,
+        ],
+        compiler_params=pltpu.CompilerParams(
+            collective_id=1, has_side_effects=True, vmem_limit_bytes=VMEM_LIMIT
+        ),
+        name="rows_gather",
+    )(rows, small)
+
+
+def exchange_kernel(count, *refs):
+    ins, outs = refs[:count], refs[count : 2 * count]
+    send, recv, own_sem = refs[2 * count :]
+    me = my_place()
+    meet_all()
+    copies = []
+    for k in range(count):
+        for step in range(1, 8):
+            place, target = peer(step)
+            copy = remote(ins[k].at[place], outs[k].at[me], send.at[k, step], recv.at[k, step], target)
+            copy.start()
+            copies.append(copy)
+        own = pltpu.make_async_copy(ins[k].at[me], outs[k].at[me], own_sem.at[k])
+        own.start()
+        copies.append(own)
+    for copy in copies:
+        copy.wait()
+
+
+def exchange(values, identity):
+    count = len(values)
+    return pl.pallas_call(
+        functools.partial(exchange_kernel, count),
+        out_shape=tuple(jax.ShapeDtypeStruct(v.shape, v.dtype) for v in values),
+        in_specs=[vmem()] * count,
+        out_specs=(vmem(),) * count,
+        scratch_shapes=[
+            pltpu.SemaphoreType.DMA((count, 8)),
+            pltpu.SemaphoreType.DMA((count, 8)),
+            pltpu.SemaphoreType.DMA((count,)),
+        ],
+        compiler_params=pltpu.CompilerParams(
+            collective_id=identity, has_side_effects=True, vmem_limit_bytes=VMEM_LIMIT
+        ),
+        name="exchange",
+    )(*values)
+
+
+def cube_sum_kernel(part, total, got0, got1, got2, held0, held1, send, recv):
+    bits = my_bits()
+    meet_all()
+    started = []
+    copies = []
+    for k, order in enumerate(ORDERS):
+        start, count = COLOURS[k]
+        src = part.at[cube_index(bits, {order[0]: 1 - bits[order[0]]}, COLOURS[k])]
+        dst = got0.at[cube_index(bits, {order[0]: 0}, COLOURS[k])]
+        copy = remote(src, dst, send.at[0, k], recv.at[0, k], neighbour(order[0]))
+        copy.start()
+        copies.append(copy)
+    started += copies
+    later = []
+    for k, order in enumerate(ORDERS):
+        copies[k].wait_recv()
+        rows = pl.ds(*COLOURS[k])
+        for u in range(2):
+            for v in range(2):
+                coords = {order[0]: bits[order[0]], order[1]: u, order[2]: v}
+                landed = {order[0]: 0, order[1]: u, order[2]: v}
+                here = (coords[2], coords[1], coords[0], rows)
+                there = (landed[2], landed[1], landed[0], rows)
+                held0[u, v, rows] = (part[here].astype(f32) + got0[there].astype(f32)).astype(bf16)
+        copy = remote(
+            held0.at[1 - bits[order[1]], :, rows], got1.at[:, rows], send.at[1, k], recv.at[1, k], neighbour(order[1])
+        )
+        copy.start()
+        later.append(copy)
+    started += later
+    last = []
+    for k, order in enumerate(ORDERS):
+        later[k].wait_recv()
+        rows = pl.ds(*COLOURS[k])
+        for v in range(2):
+            held1[v, rows] = (held0[bits[order[1]], v, rows].astype(f32) + got1[v, rows].astype(f32)).astype(bf16)
+        copy = remote(
+            held1.at[1 - bits[order[2]], rows], got2.at[rows], send.at[2, k], recv.at[2, k], neighbour(order[2])
+        )
+        copy.start()
+        last.append(copy)
+    started += last
+    for k, order in enumerate(ORDERS):
+        last[k].wait_recv()
+        rows = pl.ds(*COLOURS[k])
+        total[rows] = held1[bits[order[2]], rows].astype(f32) + got2[rows].astype(f32)
+    for copy in started:
+        copy.wait_send()
+
+
+def cube_sum(part, identity):
+    width = part.shape[-1]
+    return pl.pallas_call(
+        cube_sum_kernel,
+        out_shape=jax.ShapeDtypeStruct((256, width), f32),
+        in_specs=[vmem()],
+        out_specs=vmem(),
+        scratch_shapes=[
+            pltpu.VMEM((2, 2, 2, 256, width), bf16),
+            pltpu.VMEM((2, 256, width), bf16),
+            pltpu.VMEM((256, width), bf16),
+            pltpu.VMEM((2, 2, 256, width), bf16),
+            pltpu.VMEM((2, 256, width), bf16),
+            pltpu.SemaphoreType.DMA((3, 3)),
+            pltpu.SemaphoreType.DMA((3, 3)),
+        ],
+        compiler_params=pltpu.CompilerParams(
+            collective_id=identity, has_side_effects=True, vmem_limit_bytes=VMEM_LIMIT
+        ),
+        name="cube_sum",
+    )(part)
+
+
+def lanes(shape):
+    return lax.broadcasted_iota(jnp.int32, shape, len(shape) - 1)
+
+
+def turned(u):
+    low = lax.rem(lanes(u.shape), 64) < 32
+    return jnp.where(low, -pltpu.roll(u, 96, 1), pltpu.roll(u, 32, 1))
+
+
+def two_heads(q):
+    low = lanes(q.shape) < 64
+    return jnp.concatenate([jnp.where(low, q, 0.0), jnp.where(low, pltpu.roll(q, 64, 1), 0.0)], 0)
+
+
+def two_heads_high(g):
+    high = lanes(g.shape) >= 64
+    return jnp.concatenate([jnp.where(high, pltpu.roll(g, 64, 1), 0.0), jnp.where(high, g, 0.0)], 0)
+
+
+def block_probability(q_ref, kv_ref, seg_col, seg_row, s, i):
+    first = max(0, i - 4) * 128
+    count = (i + 1) * 128 - first
+    q2 = two_heads(q_ref[s, pl.ds(i * 128, 128)].astype(f32))
+    kv = kv_ref[s, pl.ds(first, count)]
+    raw = dot_last((q2 * 0.125).astype(bf16), kv)
+    q_place = i * 128 + lax.broadcasted_iota(jnp.int32, (128, count), 0)
+    k_place = first + lanes((128, count))
+    q_doc = seg_col[s, pl.ds(i * 128, 128)]
+    k_doc = seg_row[s, :, pl.ds(first, count)]
+    allowed = (q_place >= k_place) & (q_doc == k_doc)
+    allowed = jnp.concatenate([allowed, allowed], 0)
+    masked = jnp.where(allowed, raw, masked_out)
+    top = jnp.max(masked, -1, keepdims=True)
+    weight = jnp.exp(masked - top)
+    probability = weight * (1.0 / jnp.sum(weight, -1, keepdims=True))
+    return first, count, q2, kv, probability
+
+
+def attention_kernel(tok, w, gain, seg_col, seg_row, cosine, sine, attn_out, q_out, kv_out, mix_out):
+    gain_row = gain[...]
+
+    def project(j, carry):
+        rows = pl.ds(pl.multiple_of(j * 128, 128), 128)
+        x = tok[j].astype(f32)
+        scale = lax.rsqrt(jnp.mean(x * x, -1, keepdims=True) + epsilon)
+        attn_in = (x * scale * gain_row).astype(bf16)
+        attn_out[j] = attn_in
+        both = dot(attn_in, w[...])
+        c = cosine[rows]
+        n = sine[rows]
+        c2 = jnp.concatenate([c, c], 0)
+        n2 = jnp.concatenate([n, n], 0)
+        q = both[:, :128]
+        kv = both[:, 128:]
+        q = (q * c2 + turned(q) * n2).astype(bf16)
+        kv = jnp.where(lanes(kv.shape) < 64, kv * c2 + turned(kv) * n2, kv).astype(bf16)
+        for s in range(2):
+            q_out[s, rows] = q[s * 128 : (s + 1) * 128]
+            kv_out[s, rows] = kv[s * 128 : (s + 1) * 128]
+        return carry
+
+    lax.fori_loop(0, 8, project, 0)
+
+    def attend(s, carry):
+        for i in range(8):
+            first, count, q2, kv, probability = block_probability(q_out, kv_out, seg_col, seg_row, s, i)
+            mixed = dot(probability.astype(bf16), kv)
+            low = lanes((128, 128)) < 64
+            mix_out[i, s] = jnp.where(low, pltpu.roll(mixed[:128], 64, 1), mixed[128:]).astype(bf16)
+        return carry
+
+    lax.fori_loop(0, 2, attend, 0)
+
+
+def attention(tok, w, gain, seg_col, seg_row, cosine, sine):
+    width = tok.shape[-1]
+    return pl.pallas_call(
+        attention_kernel,
+        out_shape=(
+            jax.ShapeDtypeStruct((8, 256, width), bf16),
+            jax.ShapeDtypeStruct((2, 1024, 128), bf16),
+            jax.ShapeDtypeStruct((2, 1024, 128), bf16),
+            jax.ShapeDtypeStruct((8, 2, 128, 128), bf16),
+        ),
+        in_specs=[vmem()] * 7,
+        out_specs=(vmem(),) * 4,
+        compiler_params=pltpu.CompilerParams(vmem_limit_bytes=VMEM_LIMIT),
+        name="attention",
+    )(tok, w, gain, seg_col, seg_row, cosine, sine)
+
+
+def attention_back_kernel(
+    mix_grad, attn_in, q_in, kv_in, seg_col, seg_row, cosine, sine, gq_out, gkv_out, w_grad, kv_sum, g_all
+):
+    def attend(s, carry):
+        kv_sum[...] = jnp.zeros_like(kv_sum)
+        for i in range(8):
+            first, count, q2, kv, probability = block_probability(q_in, kv_in, seg_col, seg_row, s, i)
+            g2 = two_heads_high(mix_grad[i, s].astype(f32)).astype(bf16)
+            prob_grad = dot_last(g2, kv)
+            delta = jnp.sum(probability * prob_grad, -1, keepdims=True)
+            score_grad = (probability * (prob_grad - delta) * 0.125).astype(bf16)
+            dq = dot(score_grad, kv)
+            keys = pl.ds(first, count)
+            kv_sum[keys] += dot_first(score_grad, q2.astype(bf16)) + dot_first(probability.astype(bf16), g2)
+            low = lanes((128, 128)) < 64
+            dq = jnp.where(low, dq[:128], pltpu.roll(dq[128:], 64, 1))
+            rows = pl.ds(i * 128, 128)
+            dq = (dq * cosine[rows] - turned(dq) * sine[rows]).astype(bf16)
+            gq_out[i, s] = dq
+            g_all[i, s, :, 0:128] = dq
+        for i in range(8):
+            rows = pl.ds(i * 128, 128)
+            dkv = kv_sum[rows]
+            low = lanes((128, 128)) < 64
+            dkv = jnp.where(low, dkv * cosine[rows] - turned(dkv) * sine[rows], dkv).astype(bf16)
+            gkv_out[i, s] = dkv
+            g_all[i, s, :, 128:256] = dkv
+        return carry
+
+    lax.fori_loop(0, 2, attend, 0)
+    w_grad[...] = dot_first(attn_in[...].reshape(2048, attn_in.shape[-1]), g_all[...].reshape(2048, 256)).astype(bf16)
+
+
+def attention_back(mix_grad, attn_in, q, kv, seg_col, seg_row, cosine, sine):
+    width = attn_in.shape[-1]
+    return pl.pallas_call(
+        attention_back_kernel,
+        out_shape=(
+            jax.ShapeDtypeStruct((8, 2, 128, 128), bf16),
+            jax.ShapeDtypeStruct((8, 2, 128, 128), bf16),
+            jax.ShapeDtypeStruct((width, 256), bf16),
+        ),
+        in_specs=[vmem()] * 8,
+        out_specs=(vmem(),) * 3,
+        scratch_shapes=[pltpu.VMEM((1024, 128), f32), pltpu.VMEM((8, 2, 128, 256), bf16)],
+        compiler_params=pltpu.CompilerParams(vmem_limit_bytes=VMEM_LIMIT),
+        name="attention_back",
+    )(mix_grad, attn_in, q, kv, seg_col, seg_row, cosine, sine)
+
+
+def turned_place(m, order):
+    return sum(((m >> link) & 1) << s for s, link in enumerate(order))
+
+
+def load_weight(dst, own_half, other_half, order, sem):
+    me = my_place()
+    core = lax.rem(lax.axis_index("group"), 2)
+    copies = []
+    for i in range(8):
+        entry = turned_place(me ^ i, order)
+        for half, src in ((core, own_half), (1 - core, other_half)):
+            copy = pltpu.make_async_copy(src.at[entry], dst.at[pl.ds(i * 128 + half * 64, 64)], sem)
+            copy.start()
+            copies.append(copy)
+    return copies
+
+
+def route_kernel(mix, tok, wo_own, wo_other, gain, router, routes, residual_out, moe_in_out, weights_out, wo, sem):
+    copies = load_weight(wo, wo_own, wo_other, ORDERS[0], sem)
+    for copy in copies:
+        copy.wait()
+    residual = tok[...].astype(f32) + dot(mix[...], wo[...])
+    residual_out[...] = residual
+    scale = lax.rsqrt(jnp.mean(residual * residual, -1, keepdims=True) + epsilon)
+    moe_in = (residual * scale * gain[...]).astype(bf16)
+    moe_in_out[...] = moe_in
+    logits = lax.dot_general(router[...], moe_in, (((0,), (1,)), ((), ())), preferred_element_type=f32)
+    experts = lax.broadcasted_iota(jnp.int32, logits.shape, 0)
+    picked = [
+        jnp.sum(jnp.where(experts == routes[pl.ds(k, 1)], logits, 0.0), 0, keepdims=True) for k in range(TOP)
+    ]
+    picked = jnp.concatenate(picked, 0)
+    weight = jnp.exp(picked - jnp.max(picked, 0, keepdims=True))
+    weights_out[...] = weight / jnp.sum(weight, 0, keepdims=True)
+
+
+def route(mix, tok, wo_own, wo_other, gain, router, routes):
+    width = tok.shape[-1]
+    return pl.pallas_call(
+        route_kernel,
+        out_shape=(
+            jax.ShapeDtypeStruct((256, width), f32),
+            jax.ShapeDtypeStruct((256, width), bf16),
+            jax.ShapeDtypeStruct((8, 256), f32),
+            jax.ShapeDtypeStruct((width, width), bf16),
+        ),
+        in_specs=[vmem(), vmem(), anywhere(), anywhere(), vmem(), vmem(), vmem()],
+        out_specs=(vmem(),) * 4,
+        scratch_shapes=[pltpu.SemaphoreType.DMA],
+        compiler_params=pltpu.CompilerParams(vmem_limit_bytes=VMEM_LIMIT),
+        name="route",
+    )(mix, tok, wo_own, wo_other, gain, router, routes)
+
+
+def load_rows(dst, pieces, sem):
+    me = my_place()
+    copies = []
+    for i in range(8):
+        for k, (start, count) in enumerate(COLOURS):
+            entry = turned_place(me ^ i, ORDERS[k])
+            copy = pltpu.make_async_copy(pieces[k].at[entry], dst.at[i, pl.ds(start, count)], sem)
+            copy.start()
+            copies.append(copy)
+    return copies
+
+
+SLOT = 4 * CAPH
+SPAN = 512
+
+
+def choose_rows(routes, weights, upper, plain, scaled, first_expert, block):
+    columns = pl.ds(pl.multiple_of(block * SPAN, SPAN), SPAN)
+    chosen = routes[:, columns]
+    weight = weights[:, columns]
+    masks = [jnp.max((chosen == first_expert + e).astype(f32), 0, keepdims=True) for e in range(4)]
+    mask = jnp.concatenate(masks + [jnp.zeros((4, SPAN), f32)], 0)
+    rank = dot(mask.astype(bf16), upper[...])
+    slots = lax.broadcasted_iota(jnp.int32, (SLOT, SPAN), 0).astype(f32)
+    for e in range(4):
+        share = jnp.sum(jnp.where(chosen == first_expert + e, weight, 0.0), 0, keepdims=True)
+        hit = (slots == rank[e : e + 1]) & (mask[e : e + 1] > 0.0)
+        plain[block, e * SLOT : (e + 1) * SLOT] = jnp.where(hit, 1.0, 0.0).astype(bf16)
+        scaled[block, e * SLOT : (e + 1) * SLOT] = jnp.where(hit, share, 0.0).astype(bf16)
+
+
+def dispatch(x, c, plain, scaled, rows, pair_grad, block):
+    pair = pl.ds(block * 2, 2)
+    width = x.shape[-1]
+    rows[block] = dot(plain[block], x[pair].reshape(SPAN, width)).astype(bf16)
+    pair_grad[block] = dot(scaled[block], c[pair].reshape(SPAN, width)).astype(bf16)
+
+
+def weight_copies(e, slot, gate_hbm, up_hbm, down_hbm, gate, up, down, sem):
+    return [
+        pltpu.make_async_copy(gate_hbm.at[e], gate.at[slot], sem.at[slot, 0]),
+        pltpu.make_async_copy(up_hbm.at[e], up.at[slot], sem.at[slot, 1]),
+        pltpu.make_async_copy(down_hbm.at[e], down.at[slot], sem.at[slot, 2]),
+    ]
+
+
+def expert_inner(rows_e, pair_e, gate_w, up_w, down_w):
+    gate_val = dot(rows_e, gate_w)
+    up_val = dot(rows_e, up_w)
+    sig = 1.0 / (1.0 + jnp.exp(-gate_val))
+    silu = gate_val * sig
+    hidden = (silu * up_val).astype(bf16)
+    hidden_grad = dot_last(pair_e, down_w)
+    gate_grad = (hidden_grad * up_val * sig * (1.0 + gate_val * (1.0 - sig))).astype(bf16)
+    up_grad = (hidden_grad * silu).astype(bf16)
+    return hidden, gate_grad, up_grad
+
+
+def experts_kernel(
+    x_hbm, c0, c1, c2, routes, weights, upper, gate_hbm, up_hbm, down_hbm,
+    out_part, in_part, p_out, rows_out, pair_out, hidden_out, gate_out, up_out,
+    x, c, plain, scaled, rows, pair_grad, expert_out, pair_in, p_col,
+    gate, up, down, hid_buf, gg_buf, ug_buf, part_buf,
+    sem_x, sem_c, sem_w, sem_rows, sem_h, sem_part,
+):
+    first = my_place() * 4
+    width = x.shape[-1]
+    load_x = pltpu.make_async_copy(x_hbm, x, sem_x)
+    load_x.start()
+    load_c = load_rows(c, (c0, c1, c2), sem_c)
+    for copy in weight_copies(0, 0, gate_hbm, up_hbm, down_hbm, gate, up, down, sem_w):
+        copy.start()
+
+    def build(block, carry):
+        choose_rows(routes, weights, upper, plain, scaled, first, block)
+        return carry
+
+    lax.fori_loop(0, 4, build, 0)
+    load_x.wait()
+    for copy in load_c:
+        copy.wait()
+
+    def send(block, carry):
+        dispatch(x, c, plain, scaled, rows, pair_grad, block)
+        return carry
+
+    lax.fori_loop(0, 4, send, 0)
+    keep = [
+        pltpu.make_async_copy(rows, rows_out, sem_rows.at[0]),
+        pltpu.make_async_copy(pair_grad, pair_out, sem_rows.at[1]),
+    ]
+    for copy in keep:
+        copy.start()
+    keep_h = []
+    for e in range(4):
+        slot = e % 2
+        for copy in weight_copies(e, slot, gate_hbm, up_hbm, down_hbm, gate, up, down, sem_w):
+            copy.wait()
+        if e < 3:
+            for copy in weight_copies(e + 1, 1 - slot, gate_hbm, up_hbm, down_hbm, gate, up, down, sem_w):
+                copy.start()
+        mine = pl.ds(e * SLOT, SLOT)
+        rows_e = rows[:, mine].reshape(4 * SLOT, width)
+        pair_e = pair_grad[:, mine].reshape(4 * SLOT, width)
+        hidden, gate_grad, up_grad = expert_inner(rows_e, pair_e, gate[slot], up[slot], down[slot])
+        if e >= 2:
+            for copy in keep_h[e - 2]:
+                copy.wait()
+        hid_buf[slot] = hidden
+        gg_buf[slot] = gate_grad
+        ug_buf[slot] = up_grad
+        now = [
+            pltpu.make_async_copy(hid_buf.at[slot], hidden_out.at[e], sem_h.at[slot, 0]),
+            pltpu.make_async_copy(gg_buf.at[slot], gate_out.at[e], sem_h.at[slot, 1]),
+            pltpu.make_async_copy(ug_buf.at[slot], up_out.at[e], sem_h.at[slot, 2]),
+        ]
+        for copy in now:
+            copy.start()
+        keep_h.append(now)
+        out_e = dot(hidden, down[slot]).astype(bf16)
+        p = jnp.sum(out_e.astype(f32) * pair_e.astype(f32), -1, keepdims=True)
+        p_col[:, mine] = p.reshape(4, SLOT, 1)
+        expert_out[:, mine] = out_e.reshape(4, SLOT, width)
+        back = dot_last(gate_grad, gate[slot]) + dot_last(up_grad, up[slot])
+        pair_in[:, mine] = back.astype(bf16).reshape(4, SLOT, width)
+    for copies in keep_h[2:]:
+        for copy in copies:
+            copy.wait()
+
+    def combine(block, carry):
+        out = dot_first(scaled[block], expert_out[block]).astype(bf16)
+        part_buf[0] = out.reshape(2, 256, width)
+        first_copy = pltpu.make_async_copy(part_buf.at[0], out_part.at[pl.ds(block * 2, 2)], sem_part.at[0])
+        first_copy.start()
+        back = dot_first(plain[block], pair_in[block]).astype(bf16)
+        part_buf[1] = back.reshape(2, 256, width)
+        second_copy = pltpu.make_async_copy(part_buf.at[1], in_part.at[pl.ds(block * 2, 2)], sem_part.at[1])
+        second_copy.start()
+        for e in range(4):
+            mine = pl.ds(e * SLOT, SLOT)
+            p = jnp.sum(plain[block, mine].astype(f32) * p_col[block, mine], 0, keepdims=True)
+            p_out[block * 2, pl.ds(e, 1)] = p[:, :256]
+            p_out[block * 2 + 1, pl.ds(e, 1)] = p[:, 256:]
+        first_copy.wait()
+        second_copy.wait()
+        return carry
+
+    p_out[...] = jnp.zeros_like(p_out)
+    lax.fori_loop(0, 4, combine, 0)
+    for copy in keep:
+        copy.wait()
+
+
+def experts(x, c, routes, weights, upper, gate_w, up_w, down_w):
+    width = x.shape[-1]
+    ff = gate_w.shape[-1]
+    taken = 4 * SLOT
+    return pl.pallas_call(
+        experts_kernel,
+        out_shape=(
+            jax.ShapeDtypeStruct((8, 256, width), bf16),
+            jax.ShapeDtypeStruct((8, 256, width), bf16),
+            jax.ShapeDtypeStruct((8, 8, 256), f32),
+            jax.ShapeDtypeStruct((4, taken, width), bf16),
+            jax.ShapeDtypeStruct((4, taken, width), bf16),
+            jax.ShapeDtypeStruct((4, taken, ff), bf16),
+            jax.ShapeDtypeStruct((4, taken, ff), bf16),
+            jax.ShapeDtypeStruct((4, taken, ff), bf16),
+        ),
+        in_specs=[anywhere()] * 4 + [vmem()] * 3 + [anywhere()] * 3,
+        out_specs=(anywhere(), anywhere(), vmem()) + (anywhere(),) * 5,
+        scratch_shapes=[
+            pltpu.VMEM((8, 256, width), bf16),
+            pltpu.VMEM((8, 256, width), bf16),
+            pltpu.VMEM((4, taken, SPAN), bf16),
+            pltpu.VMEM((4, taken, SPAN), bf16),
+            pltpu.VMEM((4, taken, width), bf16),
+            pltpu.VMEM((4, taken, width), bf16),
+            pltpu.VMEM((4, taken, width), bf16),
+            pltpu.VMEM((4, taken, width), bf16),
+            pltpu.VMEM((4, taken, 1), f32),
+            pltpu.VMEM((2, width, ff), bf16),
+            pltpu.VMEM((2, width, ff), bf16),
+            pltpu.VMEM((2, ff, width), bf16),
+            pltpu.VMEM((2, taken, ff), bf16),
+            pltpu.VMEM((2, taken, ff), bf16),
+            pltpu.VMEM((2, taken, ff), bf16),
+            pltpu.VMEM((2, 2, 256, width), bf16),
+            pltpu.SemaphoreType.DMA,
+            pltpu.SemaphoreType.DMA,
+            pltpu.SemaphoreType.DMA((2, 3)),
+            pltpu.SemaphoreType.DMA((2,)),
+            pltpu.SemaphoreType.DMA((2, 3)),
+            pltpu.SemaphoreType.DMA((2,)),
+        ],
+        compiler_params=pltpu.CompilerParams(vmem_limit_bytes=VMEM_LIMIT),
+        name="experts",
+    )(x, *c, routes, weights, upper, gate_w, up_w, down_w)
+
+
+def expert_weights_kernel(
+    x0, x1, x2, c0, c1, c2, routes, weights, upper, gate_hbm, up_hbm, down_hbm,
+    rows_hbm, pair_hbm, hidden_hbm, gg_hbm, ug_hbm,
+    gate_grad_out, up_grad_out, down_grad_out,
+    x, c, plain, scaled, rows, pair_grad, gate, up, down,
+    both_rows, both_pair, both_hidden, both_gate, gate_buf, up_buf, down_buf,
+    sem_x, sem_w, sem_own, sem_out,
+):
+    first = my_place() * 4
+    side = lax.axis_index("group") // 2
+    other = 1 - side
+    width = x.shape[-1]
+    ff = gate.shape[-1]
+    load = load_rows(x, (x0, x1, x2), sem_x.at[0]) + load_rows(c, (c0, c1, c2), sem_x.at[1])
+    for copy in weight_copies(0, 0, gate_hbm, up_hbm, down_hbm, gate, up, down, sem_w):
+        copy.start()
+
+    def build(block, carry):
+        choose_rows(routes, weights, upper, plain, scaled, first, block)
+        return carry
+
+    lax.fori_loop(0, 4, build, 0)
+    for copy in load:
+        copy.wait()
+
+    def send(block, carry):
+        dispatch(x, c, plain, scaled, rows, pair_grad, block)
+        return carry
+
+    lax.fori_loop(0, 4, send, 0)
+    taken = 4 * SLOT
+    pending = []
+    for e in range(4):
+        slot = e % 2
+        mine = pl.ds(e * SLOT, SLOT)
+        own = [
+            pltpu.make_async_copy(rows_hbm.at[:, mine], both_rows.at[side], sem_own.at[0]),
+            pltpu.make_async_copy(pair_hbm.at[:, mine], both_pair.at[side], sem_own.at[1]),
+            pltpu.make_async_copy(hidden_hbm.at[e], both_hidden.at[side], sem_own.at[2]),
+            pltpu.make_async_copy(gg_hbm.at[e], both_gate.at[side, :, pl.ds(0, ff)], sem_own.at[3]),
+            pltpu.make_async_copy(ug_hbm.at[e], both_gate.at[side, :, pl.ds(ff, ff)], sem_own.at[4]),
+        ]
+        for copy in own:
+            copy.start()
+        for copy in weight_copies(e, slot, gate_hbm, up_hbm, down_hbm, gate, up, down, sem_w):
+            copy.wait()
+        if e < 3:
+            for copy in weight_copies(e + 1, 1 - slot, gate_hbm, up_hbm, down_hbm, gate, up, down, sem_w):
+                copy.start()
+        rows_e = rows[:, mine].reshape(taken, width)
+        pair_e = pair_grad[:, mine].reshape(taken, width)
+        hidden, gate_grad, up_grad = expert_inner(rows_e, pair_e, gate[slot], up[slot], down[slot])
+        both_rows[other] = rows_e.reshape(4, SLOT, width)
+        both_pair[other] = pair_e.reshape(4, SLOT, width)
+        both_hidden[other] = hidden
+        both_gate[other, :, 0:ff] = gate_grad
+        both_gate[other, :, ff : 2 * ff] = up_grad
+        for copy in own:
+            copy.wait()
+        if e >= 1:
+            for copy in pending:
+                copy.wait()
+        sums = dot_first(both_rows[...].reshape(2 * taken, width), both_gate[...].reshape(2 * taken, 2 * ff))
+        gate_buf[...] = sums[:, :ff].astype(bf16)
+        up_buf[...] = sums[:, ff:].astype(bf16)
+        down_buf[...] = dot_first(
+            both_hidden[...].reshape(2 * taken, ff), both_pair[...].reshape(2 * taken, width)
+        ).astype(bf16)
+        pending = [
+            pltpu.make_async_copy(gate_buf, gate_grad_out.at[e], sem_out.at[0]),
+            pltpu.make_async_copy(up_buf, up_grad_out.at[e], sem_out.at[1]),
+            pltpu.make_async_copy(down_buf, down_grad_out.at[e], sem_out.at[2]),
+        ]
+        for copy in pending:
+            copy.start()
+    for copy in pending:
+        copy.wait()
+
+
+def expert_weights(x, c, routes, weights, upper, gate_w, up_w, down_w, kept):
+    width = gate_w.shape[1]
+    ff = gate_w.shape[-1]
+    taken = 4 * SLOT
+    return pl.pallas_call(
+        expert_weights_kernel,
+        out_shape=(
+            jax.ShapeDtypeStruct(gate_w.shape, bf16),
+            jax.ShapeDtypeStruct(up_w.shape, bf16),
+            jax.ShapeDtypeStruct(down_w.shape, bf16),
+        ),
+        in_specs=[anywhere()] * 6 + [vmem()] * 3 + [anywhere()] * 8,
+        out_specs=(anywhere(),) * 3,
+        scratch_shapes=[
+            pltpu.VMEM((8, 256, width), bf16),
+            pltpu.VMEM((8, 256, width), bf16),
+            pltpu.VMEM((4, taken, SPAN), bf16),
+            pltpu.VMEM((4, taken, SPAN), bf16),
+            pltpu.VMEM((4, taken, width), bf16),
+            pltpu.VMEM((4, taken, width), bf16),
+            pltpu.VMEM((2, width, ff), bf16),
+            pltpu.VMEM((2, width, ff), bf16),
+            pltpu.VMEM((2, ff, width), bf16),
+            pltpu.VMEM((2, 4, SLOT, width), bf16),
+            pltpu.VMEM((2, 4, SLOT, width), bf16),
+            pltpu.VMEM((2, taken, ff), bf16),
+            pltpu.VMEM((2, taken, 2 * ff), bf16),
+            pltpu.VMEM((width, ff), bf16),
+            pltpu.VMEM((width, ff), bf16),
+            pltpu.VMEM((ff, width), bf16),
+            pltpu.SemaphoreType.DMA((2,)),
+            pltpu.SemaphoreType.DMA((2, 3)),
+            pltpu.SemaphoreType.DMA((5,)),
+            pltpu.SemaphoreType.DMA((3,)),
+        ],
+        compiler_params=pltpu.CompilerParams(vmem_limit_bytes=VMEM_LIMIT),
+        name="expert_weights",
+    )(*x, *c, routes, weights, upper, gate_w, up_w, down_w, *kept)
+
+
+def norm_back(values, gain, grad):
+    scale = lax.rsqrt(jnp.mean(values * values, -1, keepdims=True) + epsilon)
+    inner = grad * gain
+    along = jnp.mean(values * inner, -1, keepdims=True)
+    out = scale * inner - values * (scale * scale * scale * along)
+    gain_grad = jnp.sum(grad * values * scale, 0, keepdims=True)
+    return out, gain_grad
+
+
+def route_back_kernel(
+    cot, residual, moe_in_sum, p_all, routes, weights, router, moe_in, gain, wo, mix,
+    residual_grad_out, mix_grad_out, router_grad, gain_grad_out, wo_grad,
+):
+    experts_ids = lax.broadcasted_iota(jnp.int32, (32, 256), 0)
+    dense = jnp.zeros((32, 256), f32)
+    for k in range(TOP):
+        dense = dense + jnp.where(experts_ids == routes[pl.ds(k, 1)], weights[pl.ds(k, 1)], 0.0)
+    p = p_all[...]
+    logit_grad = (p - dense * jnp.sum(p, 0, keepdims=True)).astype(bf16)
+    moe_in_grad = moe_in_sum[...] + lax.dot_general(
+        logit_grad, router[...], (((0,), (1,)), ((), ())), preferred_element_type=f32
+    )
+    router_grad[...] = lax.dot_general(
+        moe_in[...], logit_grad, (((0,), (1,)), ((), ())), preferred_element_type=f32
+    ).astype(bf16)
+    part, gain_grad = norm_back(residual[...], gain[...], moe_in_grad)
+    gain_grad_out[...] = gain_grad
+    residual_grad = cot[...].astype(f32) + part
+    residual_grad_out[...] = residual_grad
+    low = residual_grad.astype(bf16)
+    mix_grad = dot_last(low, wo[...]).astype(bf16)
+    for j in range(8):
+        mix_grad_out[j] = mix_grad[:, j * 128 : (j + 1) * 128].reshape(2, 128, 128)
+    wo_grad[...] = dot_first(mix[...], low).astype(bf16)
+
+
+def route_back(cot, residual, moe_in_sum, p_all, routes, weights, router, moe_in, gain, wo, mix):
+    width = cot.shape[-1]
+    return pl.pallas_call(
+        route_back_kernel,
+        out_shape=(
+            jax.ShapeDtypeStruct((256, width), f32),
+            jax.ShapeDtypeStruct((8, 2, 128, 128), bf16),
+            jax.ShapeDtypeStruct((width, 32), bf16),
+            jax.ShapeDtypeStruct((1, width), f32),
+            jax.ShapeDtypeStruct((width, width), bf16),
+        ),
+        in_specs=[vmem()] * 11,
+        out_specs=(vmem(),) * 5,
+        compiler_params=pltpu.CompilerParams(vmem_limit_bytes=VMEM_LIMIT),
+        name="route_back",
+    )(cot, residual, moe_in_sum, p_all, routes, weights, router, moe_in, gain, wo, mix)
+
+
+def token_back_kernel(
+    gq, gkv, wq_own, wq_other, wkv_own, wkv_other, tok, gain, residual_grad, token_grad, gain_grad_out, wq, wkv, sem
+):
+    copies = load_weight(wq, wq_own, wq_other, ORDERS[1], sem.at[0])
+    copies += load_weight(wkv, wkv_own, wkv_other, ORDERS[2], sem.at[1])
+    for copy in copies:
+        copy.wait()
+    grad = dot_last(gq[...], wq[...]) + dot_last(gkv[...], wkv[...])
+    part, gain_grad = norm_back(tok[...].astype(f32), gain[...], grad)
+    gain_grad_out[...] = gain_grad
+    token_grad[...] = residual_grad[...] + part
+
+
+def token_back(gq, gkv, wq, wkv, tok, gain, residual_grad):
+    width = tok.shape[-1]
+    return pl.pallas_call(
+        token_back_kernel,
+        out_shape=(jax.ShapeDtypeStruct((256, width), f32), jax.ShapeDtypeStruct((1, width), f32)),
+        in_specs=[vmem()] * 2 + [anywhere()] * 4 + [vmem()] * 3,
+        out_specs=(vmem(),) * 2,
+        scratch_shapes=[
+            pltpu.VMEM((width, width), bf16),
+            pltpu.VMEM((width, width), bf16),
+            pltpu.SemaphoreType.DMA((2,)),
+        ],
+        compiler_params=pltpu.CompilerParams(vmem_limit_bytes=VMEM_LIMIT),
+        name="token_back",
+    )(gq, gkv, *wq, *wkv, tok, gain, residual_grad)
+
+
+def sum_halves(value, link, axis):
+    own = jnp.asarray(axis)
+    keep = lax.dynamic_index_in_dim(value, own, 0, keepdims=False)
+    give = lax.dynamic_index_in_dim(value, 1 - own, 0, keepdims=False)
+    return (keep.astype(f32) + swap(give, link).astype(f32)).astype(bf16)
+
+
+def rows_sum_swaps(part):
+    blk = lax.axis_index("blk")
+    part = sum_halves(part, 2, blk // 2)
+    part = sum_halves(part, 1, lax.rem(blk, 2))
+    return sum_halves(part, 0, lax.axis_index("head"))
+
+
+def rows_sum_colours(part):
+    blk = lax.axis_index("blk")
+    bits = (lax.axis_index("head"), lax.rem(blk, 2), blk // 2)
+    shares = []
+    for k, (start, count) in enumerate(COLOURS):
+        piece = part[:, :, :, start : start + count]
+        axes = {2: 0, 1: 1, 0: 2}
+        order = ORDERS[k]
+        piece = jnp.transpose(piece, tuple(axes[link] for link in order) + (3, 4))
+        for link in order:
+            piece = sum_halves(piece, link, bits[link])
+        shares.append(piece)
+    return jnp.concatenate(shares, 0)
+
+
+def group_sum(value):
+    value = (value.astype(f32) + swap(value, 4).astype(f32)).astype(bf16)
+    return value.astype(f32) + swap(value, 3).astype(f32)
+
+
+def fast_on_device(
+    tokens, segments, routes, cotangent, attn_gain, moe_gain, query_weight, key_projection_matrix,
+    value_projection_matrix, out_weight, router_weight, gate_weight, up_weight, down_weight,
+):
+    width = tokens.shape[-1]
+    core = lax.rem(lax.axis_index("group"), 2)
+    tok = tokens.reshape(256, width)
+    cot = cotangent.reshape(256, width)
+    wkv = jnp.concatenate(
+        [key_projection_matrix.reshape(128, 8, 64), value_projection_matrix.reshape(128, 8, 64)], -1
+    ).reshape(128, 1024)
+    gains = jnp.concatenate([attn_gain[None], moe_gain[None], jnp.zeros((14, 128), bf16)], 0)
+    my_routes = routes.reshape(256, TOP).T
+    tok_all, w_slice, gains_all, router_all, routes_all = front(tok, query_weight, wkv, gains, router_weight, my_routes)
+    attn_gain_row = gains_all[0:1].astype(f32)
+    moe_gain_row = gains_all[1:2].astype(f32)
+    frequency = rope_base ** (-(jnp.arange(128) % 32).astype(f32) * 2.0 / 64)
+    angle = jnp.arange(1024, dtype=f32)[:, None] * frequency[None, :]
+    cosine, sine = jnp.cos(angle), jnp.sin(angle)
+    seg_col, seg_row = segments[:, :, None], segments[:, None, :]
+
+    tok_done, cot_later, wo_later, wq_later, wkv_later = lax.optimization_barrier(
+        (tok_all, cot, out_weight, query_weight, wkv)
+    )
+
+    def weight_halves(weight, order):
+        mine = lax.dynamic_slice_in_dim(weight, core * 64, 64, 0)
+        own = gather_swaps(mine, order)
+        return own, swap(own, 4)
+
+    wo_halves = weight_halves(wo_later, ORDERS[0])
+    wq_halves = weight_halves(wq_later, ORDERS[1])
+    wkv_halves = weight_halves(wkv_later, ORDERS[2])
+    cot_all = gather_rows(cot_later)
+    cot_mirror = gather_rows(swap(cot_later, 3))
+    routes_mirror = swap(routes_all, 3)
+
+    attn_in, q, kv, mix = attention(
+        tok_done.reshape(8, 256, width), w_slice, attn_gain_row, seg_col, seg_row, cosine, sine
+    )
+    (mix_rows,) = exchange((mix,), 2)
+    attn_mix = jnp.transpose(mix_rows, (1, 2, 0, 3)).reshape(256, 1024)
+    residual, moe_in, weights, wo = route(attn_mix, tok, *wo_halves, moe_gain_row, router_all, my_routes)
+    moe_all, weights_all = rows_gather(moe_in, weights)
+    moe_mirror = gather_rows(swap(moe_in, 3))
+    weights_mirror = swap(weights_all, 3)
+    places = jnp.arange(SPAN)
+    upper = (places[:, None] < places[None, :]).astype(bf16)
+    out_part, in_part, p_part, *kept = experts(
+        moe_all.reshape(8, 256, width), cot_all, routes_all, weights_all, upper, gate_weight, up_weight, down_weight
+    )
+    in_sum = cube_sum(in_part.reshape(2, 2, 2, 256, width), 3)
+    (p_rows,) = exchange((p_part,), 4)
+    p_all = p_rows[:, :4].reshape(32, 256)
+    out_sum = rows_sum_colours(out_part.reshape(2, 2, 2, 256, width))
+    mixed = (residual + out_sum.astype(f32)).astype(bf16).reshape(tokens.shape)
+    residual_grad, mix_grad, router_grad, moe_gain_grad, wo_grad = route_back(
+        cot, residual, in_sum, p_all, my_routes, weights, router_all, moe_in, moe_gain_row, wo, attn_mix
+    )
+    (mix_grad_rows,) = exchange((mix_grad,), 5)
+    gq, gkv, w_grad = attention_back(mix_grad_rows_order(mix_grad_rows), attn_in, q, kv, seg_col, seg_row, cosine, sine)
+    gq_rows, gkv_rows = exchange((gq, gkv), 6)
+    gq_rows = jnp.transpose(gq_rows, (1, 2, 0, 3)).reshape(256, 1024)
+    gkv_rows = jnp.transpose(gkv_rows, (1, 2, 0, 3)).reshape(256, 1024)
+    token_grad, attn_gain_grad = token_back(
+        gq_rows, gkv_rows, wq_halves, wkv_halves, tok, attn_gain_row, residual_grad
+    )
+    gate_part, up_part, down_part = expert_weights(
+        moe_mirror, cot_mirror, routes_mirror, weights_mirror, upper, gate_weight, up_weight, down_weight, kept
+    )
+    expert_grads = tuple(part.astype(f32) + swap(part, 4).astype(f32) for part in (gate_part, up_part, down_part))
+    (w_rows,) = exchange((w_grad.reshape(8, 128, 256),), 7)
+    w_sum = group_sum(jnp.transpose(w_rows, (1, 0, 2)))
+    query_grad = w_sum[:, :, :128].reshape(128, 1024)
+    key_grad = w_sum[:, :, 128:192].reshape(128, 512)
+    value_grad = w_sum[:, :, 192:].reshape(128, 512)
+    wo_sum = group_sum(rows_sum_swaps(wo_grad.reshape(2, 2, 2, 128, 1024)))
+    small = jnp.concatenate(
+        [router_grad, moe_gain_grad.reshape(1024, 1).astype(bf16), attn_gain_grad.reshape(1024, 1).astype(bf16)], 1
+    )
+    small_sum = group_sum(rows_sum_swaps(small.reshape(2, 2, 2, 128, 34)))
+    return (
+        mixed, token_grad.reshape(tokens.shape), small_sum[:, 33], small_sum[:, 32], query_grad, key_grad, value_grad,
+        wo_sum, small_sum[:, :32], *expert_grads,
+    )
+
+
+def mix_grad_rows_order(rows):
+    return rows
+
+
+def fits(mesh):
+    return dict(mesh.shape) == {"group": 4, "blk": 4, "head": 2}
+
+
 def solution(mesh):
     placed = (
         P("group", ("blk", "head"), None),
@@ -452,7 +1524,7 @@
         P(("blk", "head"), None, None),
     )
     return jax.shard_map(
-        on_device,
+        fast_on_device if fits(mesh) else on_device,
         mesh=mesh,
         in_specs=placed,
         out_specs=(

time: 1520 us -> 612 us (0.40)
  waiting for transfers between devices: 798 us -> 107 us
  Pallas kernels: 0 us -> 316 us
  blocking collectives: 302 us -> 0 us
  local copies, waits for them, and re-layouts: 166 us -> 42.1 us
  matrix products: 112 us -> 0 us
  starting transfers between devices: 26.2 us -> 70.8 us
    psum x1 -> x0, waiting for transfers between devices: 421 us -> none  [on_device(): lax.psum(query_shard.astype(jnp.bfloat16), 'group').astype(jnp.float32)]
    pallas_call x0 -> x15, Pallas kernels: none -> 316 us  [the longest x1 54.1 us: experts(): pl.pallas_call(experts_kernel, out_shape=(jax.ShapeDtypeStruct((8, 256, w...]
    reduce_scatter x6 -> x0, waiting for transfers between devices: 168 us -> none  [the longest x1 50.3 us: on_device(): lax.psum_scatter(query_weight_grad.astype(jnp.bfloat16), ('blk', 'head'),...]
    all_to_all x6 -> x0, blocking collectives: 154 us -> none  [the longest x1 59.5 us: on_device(): lax.all_to_all(outgoing, ('blk', 'head'), split_axis=0, concat_axis=1, ti...]
    all_gather x3 -> x0, blocking collectives: 122 us -> none  [the longest x1 77.9 us: on_device(): lax.all_gather(router_weight, ('blk', 'head'), axis=0, tiled=True)]
    dot_general x42 -> x0, matrix products: 112 us -> none  [the longest x1 8.72 us: on_device(): jnp.einsum('enf,end->efd', hidden_low, grad_arrived, preferred_element_ty...]
    ppermute x0 -> x67, waiting for transfers between devices: none -> 107 us  [swap(): return lax.ppermute(value, axis, [(i, i ^ step) for i in range(count)])]
    all_gather x6 -> x0, waiting for transfers between devices: 105 us -> none  [the longest x1 28.8 us: on_device(): lax.all_gather(key_split, 'blk', axis=1, tiled=True)]
  transfers between devices with their start and end apart: 20 -> 67, of which waited for: 17 -> 27; matrix products, arithmetic and copies ran while one was open for 7% -> 16% of each run, Pallas kernels for 0% -> 43%
where the time goes in v1:
time: 612 us; the launch traced here: 608 us
  Pallas kernels  316 us (52%)
  waiting for transfers between devices  107 us (17%)
  starting transfers between devices  70.8 us (12%)
  other arithmetic  70.4 us (12%)
  local copies, waits for them, and re-layouts  42.1 us (7%)
    ppermute x67, waiting for transfers between devices, swap(): return lax.ppermute(value, axis, [(i, i ^ step) for i in range(count)])  107 us
    ppermute x67, starting transfers between devices, swap(): return lax.ppermute(value, axis, [(i, i ^ step) for i in range(count)])  70.8 us
    pallas_call x1, Pallas kernels, experts(): pl.pallas_call(experts_kernel, out_shape=(jax.ShapeDtypeStruct((8, 256, w...  54.1 us
    pallas_call x1, Pallas kernels, front(): pl.pallas_call(front_kernel, out_shape=(jax.ShapeDtypeStruct((2, 2, 2, 25...  52 us
    pallas_call x5, Pallas kernels, exchange(): pl.pallas_call(functools.partial(exchange_kernel, count), out_shape=tuple...  49.9 us
    pallas_call x1, Pallas kernels, expert_weights(): pl.pallas_call(expert_weights_kernel, out_shape=(jax.ShapeDtypeStruct(gat...  38 us
    pallas_call x1, Pallas kernels, cube_sum(): pl.pallas_call(cube_sum_kernel, out_shape=jax.ShapeDtypeStruct((256, widt...  36.9 us
    pallas_call x1, Pallas kernels, rows_gather(): pl.pallas_call(rows_gather_kernel, out_shape=(jax.ShapeDtypeStruct((2, 2,...  33.9 us
  transfers between devices with their start and end apart: 67, of which 27 were waited for; matrix products, arithmetic and copies ran while one was open for 16% of the time, Pallas kernels for 43%

profile of v1, /device:TPU:0, one launch (start us, length us, event | category | flops | bytes accessed | tf_op | source)
XLA Modules:
  0.0 607.5 jit_solution(11127620109039620122)
XLA Ops:
  5.1 52.0 %front.1 = (bf16[2,2,2,256,1024]{4,3,2,1,0:T(8,128)(2,1)}, bf16[1024,256]{1,0:T(8,128)(2,1)}, bf16[16,1024]{1,0:T(8,128)(2,1)}, bf16[1024,32]{1,0:T(8,128)(2,1)}, s32[8,2048]{1,0:T(8,128)}) custom-call(bf16[256,1024]{1,0:T(8,128)(2,1)} %bitcast.162, bf16[128,1024]{1,0:T(8,128)(2,1)} %wq.1, bf16[128,1024]{1,0:T(8,128)(2,1)} %copy.57.wkv, ...), custom_call_target="tpu_custom_call" | custom-call | tf_op jit(solution)/shard_map/front/pallas_call | solution.py:601
  57.3 2.6 collective-permute-start.52
  60.9 2.0 collective-permute-start.4
  63.9 1.5 collective-permute-start.7
  68.4 2.8 fusion.10
  74.0 15.9 %attention.1 = (bf16[8,256,1024]{2,1,0:T(8,128)(2,1)}, bf16[2,1024,128]{2,1,0:T(8,128)(2,1)}, bf16[2,1024,128]{2,1,0:T(8,128)(2,1)}, bf16[8,2,128,128]{3,2,1,0:T(8,128)(2,1)}) custom-call(bf16[8,256,1024]{2,1,0:T(8,128)(2,1)} %bitcast.170, bf16[1024,256]{1,0:T(8,128)(2,1)} %get-tuple-element.57.w, f32[1,1024]{1,0:T(1,128)} %get-tuple-element.125.gain, ...), custom_call_target="tpu_custom_call" | custom-call | tf_op jit(solution)/shard_map/attention/pallas_call | solution.py:858
  90.0 9.6 %exchange.5 = bf16[8,2,128,128]{3,2,1,0:T(8,128)(2,1)} custom-call(bf16[8,2,128,128]{3,2,1,0:T(8,128)(2,1)} %get-tuple-element.59.refs_0_), custom_call_target="tpu_custom_call" | custom-call | tf_op jit(solution)/shard_map/exchange/pallas_call | solution.py:692
  105.8 2.0 collective-permute-done.26
  107.8 1.7 collective-permute-start.1
  117.1 1.8 collective-permute-done.23
  120.6 2.0 collective-permute-start.2
  122.6 3.2 collective-permute-done.8
  131.5 2.0 collective-permute-start.28
  133.5 2.1 collective-permute-done.56
  138.9 4.6 collective-permute-done.53
  149.6 4.5 collective-permute-done.60
  156.0 2.1 pad_maximum_fusion.10.wq_own
  158.2 5.5 collective-permute-done.54
  163.8 2.5 collective-permute-done.9
  166.3 1.5 collective-permute-start.61
  170.0 3.3 collective-permute-done.58
  173.3 2.1 pad_maximum_fusion.3.c1
  176.7 2.2 pad_maximum_fusion.c0
  182.6 2.4 collective-permute-done.55
  187.3 4.9 route.1
  192.2 33.9 %rows_gather.1 = (bf16[2,2,2,256,1024]{4,3,2,1,0:T(8,128)(2,1)}, f32[8,2048]{1,0:T(8,128)}) custom-call(bf16[256,1024]{1,0:T(8,128)(2,1)} %get-tuple-element.63.rows.moe_in, f32[8,256]{1,0:T(8,128)} %get-tuple-element.64.small.weights), custom_call_target="tpu_custom_call" | custom-call | tf_op jit(solution)/shard_map/rows_gather/pallas_call | solution.py:648
  226.1 54.1 %experts.1 = (bf16[8,256,1024]{2,1,0:T(8,128)(2,1)}, bf16[8,256,1024]{2,1,0:T(8,128)(2,1)}, f32[8,8,256]{2,1,0:T(8,128)}, bf16[4,576,1024]{2,1,0:T(8,128)(2,1)},...) custom-call(bf16[8,256,1024]{2,1,0:T(8,128)(2,1)} %bitcast.171, ...), custom_call_target="tpu_custom_call" | custom-call | tf_op jit(solution)/shard_map/experts/pallas_call | solution.py:1134
  280.2 36.9 %cube_sum.1.moe_in_sum = f32[256,1024]{1,0:T(8,128)} custom-call(bf16[2,2,2,256,1024]{4,3,2,1,0:T(8,128)(2,1)} %bitcast.167), custom_call_target="tpu_custom_call" | custom-call | tf_op jit(solution)/shard_map/cube_sum/pallas_call | solution.py:761
  317.1 7.1 %exchange.6 = f32[8,8,256]{2,1,0:T(8,128)} custom-call(f32[8,8,256]{2,1,0:T(8,128)} %get-tuple-element.71.refs_0_), custom_call_target="tpu_custom_call" | custom-call | tf_op jit(solution)/shard_map/exchange/pallas_call | solution.py:692
  325.7 6.0 route_back.1
  331.7 9.9 %exchange.7.mix_grad = bf16[8,2,128,128]{3,2,1,0:T(8,128)(2,1)} custom-call(bf16[8,2,128,128]{3,2,1,0:T(8,128)(2,1)} %get-tuple-element.73.refs_0_), custom_call_target="tpu_custom_call" | custom-call | tf_op jit(solution)/shard_map/exchange/pallas_call | solution.py:692
  341.6 17.5 %attention_back.1 = (bf16[8,2,128,128]{3,2,1,0:T(8,128)(2,1)}, bf16[8,2,128,128]{3,2,1,0:T(8,128)(2,1)}, bf16[1024,256]{1,0:T(8,128)(2,1)}) custom-call(bf16[8,2,128,128]{3,2,1,0:T(8,128)(2,1)} %exchange.7.mix_grad, bf16[8,256,1024]{2,1,0:T(8,128)(2,1)} %get-tuple-element.74.attn_in, bf16[2,1024,128]{2,1,0:T(8,128)(2,1)} %get-tuple-element.75.q_in, ...), custom_call_target="tpu_custom_call" | custom-call | tf_op jit(solution)/shard_map/attention_back/pallas_call | solution.py:908
  359.2 13.0 %exchange.8 = (bf16[8,2,128,128]{3,2,1,0:T(8,128)(2,1)}, bf16[8,2,128,128]{3,2,1,0:T(8,128)(2,1)}) custom-call(bf16[8,2,128,128]{3,2,1,0:T(8,128)(2,1)} %get-tuple-element.77.refs_0_, bf16[8,2,128,128]{3,2,1,0:T(8,128)(2,1)} %get-tuple-element.78.refs_1_), custom_call_target="tpu_custom_call" | custom-call | tf_op jit(solution)/shard_map/exchange/pallas_call | solution.py:692
  376.2 6.5 %token_back.1 = (f32[256,1024]{1,0:T(8,128)}, f32[1,1024]{1,0:T(1,128)}) custom-call(bf16[256,1024]{1,0:T(8,128)(2,1)} %get-tuple-element.131.gq, bf16[256,1024]{1,0:T(8,128)(2,1)} %get-tuple-element.130.gkv, bf16[8,64,1024]{2,1,0:T(8,128)(2,1)} %pad_maximum_fusion.10.wq_own, bf16[8,64,1024]{2,1,0:T(8,128)(2,1)} %collective-permute-done.25.wq_other, ...), custom_call_target="tpu_custom_call" | custom-call | tf_op jit(solution)/shard_map/token_back/pallas_call | solution.py:1365
  384.8 2.0 fusion.22
  386.8 2.1 slice.84
  388.9 4.9 collective-permute-start.42
  393.8 1.5 collective-permute-start.31
  399.8 1.7 collective-permute-start.16
  401.6 5.9 collective-permute-done.32
  411.4 10.3 %exchange.9 = bf16[8,128,256]{2,1,0:T(8,128)(2,1)} custom-call(bf16[8,128,256]{2,1,0:T(8,128)(2,1)} %bitcast.188), custom_call_target="tpu_custom_call" | custom-call | tf_op jit(solution)/shard_map/exchange/pallas_call | solution.py:692
  425.5 2.0 collective-permute-start.46
  427.4 2.0 add_convert_fusion
  433.3 3.1 collective-permute-done.49
  437.1 10.2 %collective-permute-done.43 = bf16[1,96,1024]{2,1,0:T(8,128)(2,1)S(1)} collective-permute-done((bf16[1,96,1024]{2,1,0:T(8,128)(2,1)S(1)}, bf16[1,96,1024]{2,1,0:T(8,128)(2,1)S(1)}, u32[]{:S(2)}, u32[]{:S(2)}) %collective-permute-start.43) | collective-permute-done | bytes 196640 | tf_op jit(solution)/shard_map/ppermute | solution.py:461
  448.8 2.0 collective-permute-start.44
  452.6 5.4 collective-permute-done.50
  458.0 1.7 collective-permute-start.51
  463.1 2.7 collective-permute-start.63
  467.0 5.0 collective-permute-done.48
  476.5 4.8 collective-permute-done.45
  481.3 2.8 collective-permute-start.36
  486.7 38.0 %expert_weights.1 = (bf16[4,1024,512]{2,1,0:T(8,128)(2,1)}, bf16[4,1024,512]{2,1,0:T(8,128)(2,1)}, bf16[4,512,1024]{2,1,0:T(8,128)(2,1)}) custom-call(bf16[8,96,1024]{2,1,0:T(8,128)(2,1)} %pad_maximum_fusion.1.x0, bf16[8,80,1024]{2,1,0:T(8,128)(2,1)} %pad_maximum_fusion.5.x1, bf16[8,80,1024]{2,1,0:T(8,128)(2,1)} %pad_maximum_fusion.6.x2, ...), custom_call_target="tpu_custom_call" | custom-call | tf_op jit(solution)/shard_map/expert_weights/pallas_call | solution.py:1260
  524.8 1.9 dynamic-slice_bitcast_fusion.3
  531.8 1.6 fusion
  542.4 7.0 %collective-permute-done.38 = bf16[2,128,1024]{2,1,0:T(8,128)(2,1)} collective-permute-done((bf16[2,128,1024]{2,1,0:T(8,128)(2,1)}, bf16[2,128,1024]{2,1,0:T(8,128)(2,1)}, u32[]{:S(2)}, u32[]{:S(2)}) %collective-permute-start.38) | collective-permute-done | bytes 524320 | tf_op jit(solution)/shard_map/ppermute | solution.py:461
  550.9 6.3 %collective-permute-done.14 = bf16[2,96,1024]{2,1,0:T(8,128)(2,1)S(1)} collective-permute-done((bf16[2,96,1024]{2,1,0:T(8,128)(2,1)}, bf16[2,96,1024]{2,1,0:T(8,128)(2,1)S(1)}, u32[]{:S(2)}, u32[]{:S(2)}) %collective-permute-start.14) | collective-permute-done | bytes 393248 | tf_op jit(solution)/shard_map/ppermute | solution.py:461
  557.7 7.4 %collective-permute-done.39 = bf16[128,1024]{1,0:T(8,128)(2,1)S(1)} collective-permute-done((bf16[128,1024]{1,0:T(8,128)(2,1)S(1)}, bf16[128,1024]{1,0:T(8,128)(2,1)S(1)}, u32[]{:S(2)}, u32[]{:S(2)}) %collective-permute-start.39) | collective-permute-done | bytes 262176 | tf_op jit(solution)/shard_map/ppermute | solution.py:461
  565.1 1.9 collective-permute-start.15
  567.2 3.6 collective-permute-done.15
  572.2 11.6 %collective-permute-done.41 = bf16[128,1024]{1,0:T(8,128)(2,1)S(1)} collective-permute-done((bf16[128,1024]{1,0:T(8,128)(2,1)S(1)}, bf16[128,1024]{1,0:T(8,128)(2,1)S(1)}, u32[]{:S(2)}, u32[]{:S(2)}) %collective-permute-start.41) | collective-permute-done | bytes 262176 | tf_op jit(solution)/shard_map/ppermute | solution.py:461
  584.7 7.0 %convert_add_fusion.2 = f32[4,1024,512]{2,1,0:T(8,128)} fusion(bf16[4,1024,512]{2,1,0:T(8,128)(2,1)} %collective-permute-done.64, bf16[4,1024,512]{2,1,0:T(8,128)(2,1)S(1)} %copy-done.7), kind=kLoop, calls=%fused_computation.2 | loop fusion | flops 6291456 | bytes 16777216 | tf_op jit(solution)/shard_map/add | solution.py:1484
  591.6 6.8 %convert_add_fusion.1 = f32[4,1024,512]{2,1,0:T(8,128)} fusion(bf16[4,1024,512]{2,1,0:T(8,128)(2,1)} %collective-permute-done.65, bf16[4,1024,512]{2,1,0:T(8,128)(2,1)S(1)} %copy-done.6), kind=kLoop, calls=%fused_computation.1 | loop fusion | flops 6291456 | bytes 16777216 | tf_op jit(solution)/shard_map/add | solution.py:1484
  598.5 8.9 %convert_add_fusion = f32[4,512,1024]{2,1,0:T(8,128)} fusion(bf16[4,512,1024]{2,1,0:T(8,128)(2,1)} %collective-permute-done.66, bf16[4,512,1024]{2,1,0:T(8,128)(2,1)} %get-tuple-element.97), kind=kLoop, calls=%fused_computation | loop fusion | flops 6291456 | bytes 16777216 | tf_op jit(solution)/shard_map/add | solution.py:1484
  (265 shorter events, 111.7 us)
Async XLA Ops:
  57.2 44.6 %collective-permute-start = (bf16[1,64,1024]{2,1,0:T(8,128)(2,1)S(1)}, bf16[1,64,1024]{2,1,0:T(8,128)(2,1)}, u32[]{:S(2)}, u32[]{:S(2)}) collective-permute-start(bf16[1,64,1024]{2,1,0:T(8,128)(2,1)S(1)} %dynamic-slice_bitcast_fusion.12), channel_id=1, source_target_pairs={{0,1},{1,0},{2,3},{3,2},{4,5},{5,4},{6,7},{7,6},{8,9},{9,8},{10,11... | collective-permute-start | bytes 393224 | tf_op jit(solution)/shard_map/ppermute | solution.py:461
  57.3 70.9 %collective-permute-start.52 = (bf16[256,1024]{1,0:T(8,128)(2,1)}, bf16[256,1024]{1,0:T(8,128)(2,1)}, u32[]{:S(2)}, u32[]{:S(2)}) collective-permute-start(bf16[256,1024]{1,0:T(8,128)(2,1)} %bitcast.180), channel_id=1, source_target_pairs={{0,16},{8,24},{16,0},{24,8},{1,17},{9,25},{17,1},{25,9},{2,18},{10... | collective-permute-start | bytes 1572872 | tf_op jit(solution)/shard_map/ppermute | solution.py:461
  60.9 52.2 %collective-permute-start.4 = (bf16[1,96,1024]{2,1,0:T(8,128)(2,1)S(1)}, bf16[1,96,1024]{2,1,0:T(8,128)(2,1)}, u32[]{:S(2)}, u32[]{:S(2)}) collective-permute-start(bf16[1,96,1024]{2,1,0:T(8,128)(2,1)S(1)} %slice_bitcast_fusion.2), channel_id=1, source_target_pairs={{0,1},{1,0},{2,3},{3,2},{4,5},{5,4},{6,7},{7,6},{8,9},{9,8},{10,11... | collective-permute-start | bytes 589832 | tf_op jit(solution)/shard_map/ppermute | solution.py:461
  63.9 45.6 %collective-permute-start.7 = (bf16[1,80,1024]{2,1,0:T(8,128)(2,1)S(1)}, bf16[1,80,1024]{2,1,0:T(8,128)(2,1)}, u32[]{:S(2)}, u32[]{:S(2)}) collective-permute-start(bf16[1,80,1024]{2,1,0:T(8,128)(2,1)S(1)} %get-tuple-element.123), channel_id=1, source_target_pairs={{0,2},{2,0},{4,6},{6,4},{1,3},{3,1},{5,7},{7,5},{8,10},{10,8},{12,... | collective-permute-start | bytes 491528 | tf_op jit(solution)/shard_map/ppermute | solution.py:461
  66.4 37.5 %collective-permute-start.22 = (bf16[1,64,1024]{2,1,0:T(8,128)(2,1)S(1)}, bf16[1,64,1024]{2,1,0:T(8,128)(2,1)}, u32[]{:S(2)}, u32[]{:S(2)}) collective-permute-start(bf16[1,64,1024]{2,1,0:T(8,128)(2,1)S(1)} %dynamic-slice_bitcast_fusion.11), channel_id=1, source_target_pairs={{0,2},{2,0},{4,6},{6,4},{1,3},{3,1},{5,7},{7,5},{8,10},{10,8},{12,... | collective-permute-start | bytes 393224 | tf_op jit(solution)/shard_map/ppermute | solution.py:461
  101.8 6.0 collective-permute-start.26
  103.9 7.7 %collective-permute-start.10 = (bf16[1,80,1024]{2,1,0:T(8,128)(2,1)S(1)}, bf16[1,80,1024]{2,1,0:T(8,128)(2,1)S(1)}, u32[]{:S(2)}, u32[]{:S(2)}) collective-permute-start(bf16[1,80,1024]{2,1,0:T(8,128)(2,1)S(1)} %get-tuple-element.122), channel_id=1, source_target_pairs={{0,4},{2,6},{4,0},{6,2},{1,5},{3,7},{5,1},{7,3},{8,12},{10,14},{12... | collective-permute-start | bytes 491528 | tf_op jit(solution)/shard_map/ppermute | solution.py:461
  107.8 7.2 %collective-permute-start.1 = (bf16[2,64,1024]{2,1,0:T(8,128)(2,1)S(1)}, bf16[2,64,1024]{2,1,0:T(8,128)(2,1)S(1)}, u32[]{:S(2)}, u32[]{:S(2)}) collective-permute-start(bf16[2,64,1024]{2,1,0:T(8,128)(2,1)S(1)} %pad_maximum_fusion.34), channel_id=1, source_target_pairs={{0,2},{2,0},{4,6},{6,4},{1,3},{3,1},{5,7},{7,5},{8,10},{10,8},{12,... | collective-permute-start | bytes 786440 | tf_op jit(solution)/shard_map/ppermute | solution.py:461
  109.5 9.3 %collective-permute-start.23 = (bf16[2,64,1024]{2,1,0:T(8,128)(2,1)S(1)}, bf16[2,64,1024]{2,1,0:T(8,128)(2,1)S(1)}, u32[]{:S(2)}, u32[]{:S(2)}) collective-permute-start(bf16[2,64,1024]{2,1,0:T(8,128)(2,1)S(1)} %pad_maximum_fusion.35), channel_id=1, source_target_pairs={{0,4},{2,6},{4,0},{6,2},{1,5},{3,7},{5,1},{7,3},{8,12},{10,14},{12... | collective-permute-start | bytes 786440 | tf_op jit(solution)/shard_map/ppermute | solution.py:461
  111.6 9.0 %collective-permute-start.27 = (bf16[2,64,1024]{2,1,0:T(8,128)(2,1)S(1)}, bf16[2,64,1024]{2,1,0:T(8,128)(2,1)S(1)}, u32[]{:S(2)}, u32[]{:S(2)}) collective-permute-start(bf16[2,64,1024]{2,1,0:T(8,128)(2,1)S(1)} %pad_maximum_fusion.36), channel_id=1, source_target_pairs={{0,1},{1,0},{2,3},{3,2},{4,5},{5,4},{6,7},{7,6},{8,9},{9,8},{10,11... | collective-permute-start | bytes 786440 | tf_op jit(solution)/shard_map/ppermute | solution.py:461
  113.1 12.7 %collective-permute-start.8 = (bf16[2,80,1024]{2,1,0:T(8,128)(2,1)S(1)}, bf16[2,80,1024]{2,1,0:T(8,128)(2,1)S(1)}, u32[]{:S(2)}, u32[]{:S(2)}) collective-permute-start(bf16[2,80,1024]{2,1,0:T(8,128)(2,1)S(1)} %pad_maximum_fusion.27), channel_id=1, source_target_pairs={{0,4},{2,6},{4,0},{6,2},{1,5},{3,7},{5,1},{7,3},{8,12},{10,14},{12... | collective-permute-start | bytes 983048 | tf_op jit(solution)/shard_map/ppermute | solution.py:461
  115.0 13.1 %collective-permute-start.11 = (bf16[2,80,1024]{2,1,0:T(8,128)(2,1)S(1)}, bf16[2,80,1024]{2,1,0:T(8,128)(2,1)S(1)}, u32[]{:S(2)}, u32[]{:S(2)}) collective-permute-start(bf16[2,80,1024]{2,1,0:T(8,128)(2,1)S(1)} %pad_maximum_fusion.28), channel_id=1, source_target_pairs={{0,1},{1,0},{2,3},{3,2},{4,5},{5,4},{6,7},{7,6},{8,9},{9,8},{10,11... | collective-permute-start | bytes 983048 | tf_op jit(solution)/shard_map/ppermute | solution.py:461
  118.8 12.7 %collective-permute-start.5 = (bf16[2,96,1024]{2,1,0:T(8,128)(2,1)S(1)}, bf16[2,96,1024]{2,1,0:T(8,128)(2,1)S(1)}, u32[]{:S(2)}, u32[]{:S(2)}) collective-permute-start(bf16[2,96,1024]{2,1,0:T(8,128)(2,1)S(1)} %pad_maximum_fusion.24), channel_id=1, source_target_pairs={{0,2},{2,0},{4,6},{6,4},{1,3},{3,1},{5,7},{7,5},{8,10},{10,8},{12,... | collective-permute-start | bytes 1179656 | tf_op jit(solution)/shard_map/ppermute | solution.py:461
  120.6 24.8 %collective-permute-start.2 = (bf16[4,64,1024]{2,1,0:T(8,128)(2,1)S(1)}, bf16[4,64,1024]{2,1,0:T(8,128)(2,1)S(1)}, u32[]{:S(2)}, u32[]{:S(2)}) collective-permute-start(bf16[4,64,1024]{2,1,0:T(8,128)(2,1)S(1)} %pad_maximum_fusion.21), channel_id=1, source_target_pairs={{0,4},{2,6},{4,0},{6,2},{1,5},{3,7},{5,1},{7,3},{8,12},{10,14},{12... | collective-permute-start | bytes 1572872 | tf_op jit(solution)/shard_map/ppermute | solution.py:461
  125.8 20.8 %collective-permute-start.24 = (bf16[4,64,1024]{2,1,0:T(8,128)(2,1)S(1)}, bf16[4,64,1024]{2,1,0:T(8,128)(2,1)S(1)}, u32[]{:S(2)}, u32[]{:S(2)}) collective-permute-start(bf16[4,64,1024]{2,1,0:T(8,128)(2,1)S(1)} %pad_maximum_fusion.22), channel_id=1, source_target_pairs={{0,1},{1,0},{2,3},{3,2},{4,5},{5,4},{6,7},{7,6},{8,9},{9,8},{10,11... | collective-permute-start | bytes 1572872 | tf_op jit(solution)/shard_map/ppermute | solution.py:461
  129.2 6.4 %collective-permute-start.56 = (bf16[1,80,1024]{2,1,0:T(8,128)(2,1)S(1)}, bf16[1,80,1024]{2,1,0:T(8,128)(2,1)S(1)}, u32[]{:S(2)}, u32[]{:S(2)}) collective-permute-start(bf16[1,80,1024]{2,1,0:T(8,128)(2,1)S(1)} %get-tuple-element.119), channel_id=1, source_target_pairs={{0,2},{2,0},{4,6},{6,4},{1,3},{3,1},{5,7},{7,5},{8,10},{10,8},{12,... | collective-permute-start | bytes 491528 | tf_op jit(solution)/shard_map/ppermute | solution.py:461
  129.5 8.3 %collective-permute-start.59 = (bf16[1,80,1024]{2,1,0:T(8,128)(2,1)S(1)}, bf16[1,80,1024]{2,1,0:T(8,128)(2,1)S(1)}, u32[]{:S(2)}, u32[]{:S(2)}) collective-permute-start(bf16[1,80,1024]{2,1,0:T(8,128)(2,1)S(1)} %get-tuple-element.118), channel_id=1, source_target_pairs={{0,4},{2,6},{4,0},{6,2},{1,5},{3,7},{5,1},{7,3},{8,12},{10,14},{12... | collective-permute-start | bytes 491528 | tf_op jit(solution)/shard_map/ppermute | solution.py:461
  131.5 17.2 %collective-permute-start.28 = (bf16[4,64,1024]{2,1,0:T(8,128)(2,1)S(1)}, bf16[4,64,1024]{2,1,0:T(8,128)(2,1)S(1)}, u32[]{:S(2)}, u32[]{:S(2)}) collective-permute-start(bf16[4,64,1024]{2,1,0:T(8,128)(2,1)S(1)} %pad_maximum_fusion.23), channel_id=1, source_target_pairs={{0,2},{2,0},{4,6},{6,4},{1,3},{3,1},{5,7},{7,5},{8,10},{10,8},{12,... | collective-permute-start | bytes 1572872 | tf_op jit(solution)/shard_map/ppermute | solution.py:461
  135.6 7.8 %collective-permute-start.53 = (bf16[1,96,1024]{2,1,0:T(8,128)(2,1)S(1)}, bf16[1,96,1024]{2,1,0:T(8,128)(2,1)S(1)}, u32[]{:S(2)}, u32[]{:S(2)}) collective-permute-start(bf16[1,96,1024]{2,1,0:T(8,128)(2,1)S(1)} %slice_bitcast_fusion), channel_id=1, source_target_pairs={{0,1},{1,0},{2,3},{3,2},{4,5},{5,4},{6,7},{7,6},{8,9},{9,8},{10,11... | collective-permute-start | bytes 589832 | tf_op jit(solution)/shard_map/ppermute | solution.py:461
  137.8 9.9 %collective-permute-start.57 = (bf16[2,80,1024]{2,1,0:T(8,128)(2,1)S(1)}, bf16[2,80,1024]{2,1,0:T(8,128)(2,1)S(1)}, u32[]{:S(2)}, u32[]{:S(2)}) collective-permute-start(bf16[2,80,1024]{2,1,0:T(8,128)(2,1)S(1)} %pad_maximum_fusion.31), channel_id=1, source_target_pairs={{0,4},{2,6},{4,0},{6,2},{1,5},{3,7},{5,1},{7,3},{8,12},{10,14},{12... | collective-permute-start | bytes 983048 | tf_op jit(solution)/shard_map/ppermute | solution.py:461
  143.5 10.6 %collective-permute-start.60 = (bf16[2,80,1024]{2,1,0:T(8,128)(2,1)S(1)}, bf16[2,80,1024]{2,1,0:T(8,128)(2,1)S(1)}, u32[]{:S(2)}, u32[]{:S(2)}) collective-permute-start(bf16[2,80,1024]{2,1,0:T(8,128)(2,1)S(1)} %pad_maximum_fusion.32), channel_id=1, source_target_pairs={{0,1},{1,0},{2,3},{3,2},{4,5},{5,4},{6,7},{7,6},{8,9},{9,8},{10,11... | collective-permute-start | bytes 983048 | tf_op jit(solution)/shard_map/ppermute | solution.py:461
  145.4 20.9 %collective-permute-start.9 = (bf16[4,80,1024]{2,1,0:T(8,128)(2,1)S(1)}, bf16[4,80,1024]{2,1,0:T(8,128)(2,1)S(1)}, u32[]{:S(2)}, u32[]{:S(2)}) collective-permute-start(bf16[4,80,1024]{2,1,0:T(8,128)(2,1)S(1)} %pad_maximum_fusion.15), channel_id=1, source_target_pairs={{0,1},{1,0},{2,3},{3,2},{4,5},{5,4},{6,7},{7,6},{8,9},{9,8},{10,11... | collective-permute-start | bytes 1966088 | tf_op jit(solution)/shard_map/ppermute | solution.py:461
  146.6 21.2 %collective-permute-start.12 = (bf16[4,80,1024]{2,1,0:T(8,128)(2,1)S(1)}, bf16[4,80,1024]{2,1,0:T(8,128)(2,1)S(1)}, u32[]{:S(2)}, u32[]{:S(2)}) collective-permute-start(bf16[4,80,1024]{2,1,0:T(8,128)(2,1)S(1)} %pad_maximum_fusion.16), channel_id=1, source_target_pairs={{0,2},{2,0},{4,6},{6,4},{1,3},{3,1},{5,7},{7,5},{8,10},{10,8},{12,... | collective-permute-start | bytes 1966088 | tf_op jit(solution)/shard_map/ppermute | solution.py:461
  147.7 22.4 %collective-permute-start.6 = (bf16[4,96,1024]{2,1,0:T(8,128)(2,1)S(1)}, bf16[4,96,1024]{2,1,0:T(8,128)(2,1)S(1)}, u32[]{:S(2)}, u32[]{:S(2)}) collective-permute-start(bf16[4,96,1024]{2,1,0:T(8,128)(2,1)S(1)} %pad_maximum_fusion.12), channel_id=1, source_target_pairs={{0,4},{2,6},{4,0},{6,2},{1,5},{3,7},{5,1},{7,3},{8,12},{10,14},{12... | collective-permute-start | bytes 2359304 | tf_op jit(solution)/shard_map/ppermute | solution.py:461
  148.7 15.0 %collective-permute-start.54 = (bf16[2,96,1024]{2,1,0:T(8,128)(2,1)S(1)}, bf16[2,96,1024]{2,1,0:T(8,128)(2,1)S(1)}, u32[]{:S(2)}, u32[]{:S(2)}) collective-permute-start(bf16[2,96,1024]{2,1,0:T(8,128)(2,1)S(1)} %pad_maximum_fusion.26), channel_id=1, source_target_pairs={{0,2},{2,0},{4,6},{6,4},{1,3},{3,1},{5,7},{7,5},{8,10},{10,8},{12,... | collective-permute-start | bytes 1179656 | tf_op jit(solution)/shard_map/ppermute | solution.py:461
  154.1 19.2 %collective-permute-start.58 = (bf16[4,80,1024]{2,1,0:T(8,128)(2,1)S(1)}, bf16[4,80,1024]{2,1,0:T(8,128)(2,1)S(1)}, u32[]{:S(2)}, u32[]{:S(2)}) collective-permute-start(bf16[4,80,1024]{2,1,0:T(8,128)(2,1)S(1)} %pad_maximum_fusion.19), channel_id=1, source_target_pairs={{0,1},{1,0},{2,3},{3,2},{4,5},{5,4},{6,7},{7,6},{8,9},{9,8},{10,11... | collective-permute-start | bytes 1966088 | tf_op jit(solution)/shard_map/ppermute | solution.py:461
  163.7 22.6 %collective-permute-start.3 = (bf16[8,64,1024]{2,1,0:T(8,128)(2,1)S(1)}, bf16[8,64,1024]{2,1,0:T(8,128)(2,1)S(1)}, u32[]{:S(2)}, u32[]{:S(2)}) collective-permute-start(bf16[8,64,1024]{2,1,0:T(8,128)(2,1)S(1)} %pad_maximum_fusion.9.wo_own), channel_id=1, source_target_pairs={{0,8},{8,0},{16,24},{24,16},{1,9},{9,1},{17,25},{25,17},{2,10},{10... | collective-permute-start | bytes 3145736 | tf_op jit(solution)/shard_map/ppermute | solution.py:461
  166.3 14.7 %collective-permute-start.61 = (bf16[4,80,1024]{2,1,0:T(8,128)(2,1)S(1)}, bf16[4,80,1024]{2,1,0:T(8,128)(2,1)S(1)}, u32[]{:S(2)}, u32[]{:S(2)}) collective-permute-start(bf16[4,80,1024]{2,1,0:T(8,128)(2,1)S(1)} %pad_maximum_fusion.20), channel_id=1, source_target_pairs={{0,2},{2,0},{4,6},{6,4},{1,3},{3,1},{5,7},{7,5},{8,10},{10,8},{12,... | collective-permute-start | bytes 1966088 | tf_op jit(solution)/shard_map/ppermute | solution.py:461
  167.8 17.2 %collective-permute-start.55 = (bf16[4,96,1024]{2,1,0:T(8,128)(2,1)S(1)}, bf16[4,96,1024]{2,1,0:T(8,128)(2,1)S(1)}, u32[]{:S(2)}, u32[]{:S(2)}) collective-permute-start(bf16[4,96,1024]{2,1,0:T(8,128)(2,1)S(1)} %pad_maximum_fusion.14), channel_id=1, source_target_pairs={{0,4},{2,6},{4,0},{6,2},{1,5},{3,7},{5,1},{7,3},{8,12},{10,14},{12... | collective-permute-start | bytes 2359304 | tf_op jit(solution)/shard_map/ppermute | solution.py:461
  170.0 206.2 %collective-permute-start.25 = (bf16[8,64,1024]{2,1,0:T(8,128)(2,1)}, bf16[8,64,1024]{2,1,0:T(8,128)(2,1)}, u32[]{:S(2)}, u32[]{:S(2)}) collective-permute-start(bf16[8,64,1024]{2,1,0:T(8,128)(2,1)} %pad_maximum_fusion.10.wq_own), channel_id=1, source_target_pairs={{0,8},{8,0},{16,24},{24,16},{1,9},{9,1},{17,25},{25,17},{2,10},{10... | collective-permute-start | bytes 3145736 | tf_op jit(solution)/shard_map/ppermute | solution.py:461
  173.3 202.9 %collective-permute-start.29 = (bf16[8,64,1024]{2,1,0:T(8,128)(2,1)}, bf16[8,64,1024]{2,1,0:T(8,128)(2,1)}, u32[]{:S(2)}, u32[]{:S(2)}) collective-permute-start(bf16[8,64,1024]{2,1,0:T(8,128)(2,1)} %pad_maximum_fusion.11.wkv_own), channel_id=1, source_target_pairs={{0,8},{8,0},{16,24},{24,16},{1,9},{9,1},{17,25},{25,17},{2,10},{10... | collective-permute-start | bytes 3145736 | tf_op jit(solution)/shard_map/ppermute | solution.py:461
  181.0 304.4 %collective-permute-start.62 = (s32[8,2048]{1,0:T(8,128)S(1)}, s32[8,2048]{1,0:T(8,128)}, u32[]{:S(2)}, u32[]{:S(2)}) collective-permute-start(s32[8,2048]{1,0:T(8,128)S(1)} %copy-done.20), channel_id=1, source_target_pairs={{0,16},{8,24},{16,0},{24,8},{1,17},{9,25},{17,1},{25,9},{2,18},{10... | collective-permute-start | bytes 196616 | tf_op jit(solution)/shard_map/ppermute | solution.py:461
  383.7 10.1 %collective-permute-start.30 = (bf16[2,2,128,34]{2,3,1,0:T(8,128)(2,1)S(1)}, bf16[2,2,128,34]{2,3,1,0:T(8,128)(2,1)S(1)}, u32[]{:S(2)}, u32[]{:S(2)}) collective-permute-start(bf16[2,2,128,34]{2,3,1,0:T(8,128)(2,1)S(1)} %dynamic-slice_bitcast_fusion.13), channel_id=1, source_target_pairs={{0,4},{2,6},{4,0},{6,2},{1,5},{3,7},{5,1},{7,3},{8,12},{10,14},{12... | collective-permute-start | bytes 104456 | tf_op jit(solution)/shard_map/ppermute | solution.py:461
  388.9 34.1 %collective-permute-start.42 = (bf16[256,1024]{1,0:T(8,128)(2,1)}, bf16[256,1024]{1,0:T(8,128)(2,1)}, u32[]{:S(2)}, u32[]{:S(2)}) collective-permute-start(bf16[256,1024]{1,0:T(8,128)(2,1)} %get-tuple-element.63.rows.moe_in), channel_id=1, source_target_pairs={{0,16},{8,24},{16,0},{24,8},{1,17},{9,25},{17,1},{25,9},{2,18},{10... | collective-permute-start | bytes 1572872 | tf_op jit(solution)/shard_map/ppermute | solution.py:461
  393.8 4.1 collective-permute-start.31
  396.3 34.0 %collective-permute-start.19 = (bf16[2,2,80,1024]{3,2,1,0:T(8,128)(2,1)}, bf16[2,2,80,1024]{3,2,1,0:T(8,128)(2,1)}, u32[]{:S(2)}, u32[]{:S(2)}) collective-permute-start(bf16[2,2,80,1024]{3,2,1,0:T(8,128)(2,1)} %bitcast.160), channel_id=1, source_target_pairs={{0,4},{2,6},{4,0},{6,2},{1,5},{3,7},{5,1},{7,3},{8,12},{10,14},{12... | collective-permute-start | bytes 1966088 | tf_op jit(solution)/shard_map/ppermute | solution.py:461
  397.9 9.5 %collective-permute-start.32 = (bf16[128,34]{0,1:T(8,128)(2,1)S(1)}, bf16[128,34]{0,1:T(8,128)(2,1)S(1)}, u32[]{:S(2)}, u32[]{:S(2)}) collective-permute-start(bf16[128,34]{0,1:T(8,128)(2,1)S(1)} %dynamic-slice_bitcast_fusion.15), channel_id=1, source_target_pairs={{0,1},{1,0},{2,3},{3,2},{4,5},{5,4},{6,7},{7,6},{8,9},{9,8},{10,11... | collective-permute-start | bytes 26120 | tf_op jit(solution)/shard_map/ppermute | solution.py:461
  399.8 49.0 %collective-permute-start.16 = (bf16[2,2,80,1024]{3,2,1,0:T(8,128)(2,1)}, bf16[2,2,80,1024]{3,2,1,0:T(8,128)(2,1)}, u32[]{:S(2)}, u32[]{:S(2)}) collective-permute-start(bf16[2,2,80,1024]{3,2,1,0:T(8,128)(2,1)} %dynamic-slice_bitcast_fusion.1), channel_id=1, source_target_pairs={{0,2},{2,0},{4,6},{6,4},{1,3},{3,1},{5,7},{7,5},{8,10},{10,8},{12,... | collective-permute-start | bytes 1966088 | tf_op jit(solution)/shard_map/ppermute | solution.py:461
  408.8 13.0 %collective-permute-start.34 = (bf16[128,34]{0,1:T(8,128)(2,1)S(1)}, bf16[128,34]{0,1:T(8,128)(2,1)S(1)}, u32[]{:S(2)}, u32[]{:S(2)}) collective-permute-start(bf16[128,34]{0,1:T(8,128)(2,1)S(1)} %add_convert_fusion.3), channel_id=1, source_target_pairs={{0,16},{8,24},{16,0},{24,8},{1,17},{9,25},{17,1},{25,9},{2,18},{10... | collective-permute-start | bytes 26120 | tf_op jit(solution)/shard_map/ppermute | solution.py:461
  423.0 40.2 %collective-permute-start.13 = (bf16[2,2,96,1024]{3,2,1,0:T(8,128)(2,1)}, bf16[2,2,96,1024]{3,2,1,0:T(8,128)(2,1)S(1)}, u32[]{:S(2)}, u32[]{:S(2)}) collective-permute-start(bf16[2,2,96,1024]{3,2,1,0:T(8,128)(2,1)} %bitcast.187), channel_id=1, source_target_pairs={{0,1},{1,0},{2,3},{3,2},{4,5},{5,4},{6,7},{7,6},{8,9},{9,8},{10,11... | collective-permute-start | bytes 2359304 | tf_op jit(solution)/shard_map/ppermute | solution.py:461
  425.5 7.0 %collective-permute-start.46 = (bf16[1,80,1024]{2,1,0:T(8,128)(2,1)S(1)}, bf16[1,80,1024]{2,1,0:T(8,128)(2,1)S(1)}, u32[]{:S(2)}, u32[]{:S(2)}) collective-permute-start(bf16[1,80,1024]{2,1,0:T(8,128)(2,1)S(1)} %get-tuple-element.121), channel_id=1, source_target_pairs={{0,2},{2,0},{4,6},{6,4},{1,3},{3,1},{5,7},{7,5},{8,10},{10,8},{12,... | collective-permute-start | bytes 491528 | tf_op jit(solution)/shard_map/ppermute | solution.py:461
  430.3 6.1 %collective-permute-start.49 = (bf16[1,80,1024]{2,1,0:T(8,128)(2,1)S(1)}, bf16[1,80,1024]{2,1,0:T(8,128)(2,1)S(1)}, u32[]{:S(2)}, u32[]{:S(2)}) collective-permute-start(bf16[1,80,1024]{2,1,0:T(8,128)(2,1)S(1)} %get-tuple-element.120), channel_id=1, source_target_pairs={{0,4},{2,6},{4,0},{6,2},{1,5},{3,7},{5,1},{7,3},{8,12},{10,14},{12... | collective-permute-start | bytes 491528 | tf_op jit(solution)/shard_map/ppermute | solution.py:461
  432.5 14.8 %collective-permute-start.43 = (bf16[1,96,1024]{2,1,0:T(8,128)(2,1)S(1)}, bf16[1,96,1024]{2,1,0:T(8,128)(2,1)S(1)}, u32[]{:S(2)}, u32[]{:S(2)}) collective-permute-start(bf16[1,96,1024]{2,1,0:T(8,128)(2,1)S(1)} %slice_bitcast_fusion.1), channel_id=1, source_target_pairs={{0,1},{1,0},{2,3},{3,2},{4,5},{5,4},{6,7},{7,6},{8,9},{9,8},{10,11... | collective-permute-start | bytes 589832 | tf_op jit(solution)/shard_map/ppermute | solution.py:461
  436.4 15.7 %collective-permute-start.47 = (bf16[2,80,1024]{2,1,0:T(8,128)(2,1)S(1)}, bf16[2,80,1024]{2,1,0:T(8,128)(2,1)S(1)}, u32[]{:S(2)}, u32[]{:S(2)}) collective-permute-start(bf16[2,80,1024]{2,1,0:T(8,128)(2,1)S(1)} %pad_maximum_fusion.29), channel_id=1, source_target_pairs={{0,4},{2,6},{4,0},{6,2},{1,5},{3,7},{5,1},{7,3},{8,12},{10,14},{12... | collective-permute-start | bytes 983048 | tf_op jit(solution)/shard_map/ppermute | solution.py:461
  447.3 10.6 %collective-permute-start.50 = (bf16[2,80,1024]{2,1,0:T(8,128)(2,1)S(1)}, bf16[2,80,1024]{2,1,0:T(8,128)(2,1)S(1)}, u32[]{:S(2)}, u32[]{:S(2)}) collective-permute-start(bf16[2,80,1024]{2,1,0:T(8,128)(2,1)S(1)} %pad_maximum_fusion.30), channel_id=1, source_target_pairs={{0,1},{1,0},{2,3},{3,2},{4,5},{5,4},{6,7},{7,6},{8,9},{9,8},{10,11... | collective-permute-start | bytes 983048 | tf_op jit(solution)/shard_map/ppermute | solution.py:461
  448.8 11.9 %collective-permute-start.44 = (bf16[2,96,1024]{2,1,0:T(8,128)(2,1)S(1)}, bf16[2,96,1024]{2,1,0:T(8,128)(2,1)S(1)}, u32[]{:S(2)}, u32[]{:S(2)}) collective-permute-start(bf16[2,96,1024]{2,1,0:T(8,128)(2,1)S(1)} %pad_maximum_fusion.25), channel_id=1, source_target_pairs={{0,2},{2,0},{4,6},{6,4},{1,3},{3,1},{5,7},{7,5},{8,10},{10,8},{12,... | collective-permute-start | bytes 1179656 | tf_op jit(solution)/shard_map/ppermute | solution.py:461
  452.2 19.9 %collective-permute-start.48 = (bf16[4,80,1024]{2,1,0:T(8,128)(2,1)S(1)}, bf16[4,80,1024]{2,1,0:T(8,128)(2,1)S(1)}, u32[]{:S(2)}, u32[]{:S(2)}) collective-permute-start(bf16[4,80,1024]{2,1,0:T(8,128)(2,1)S(1)} %pad_maximum_fusion.17), channel_id=1, source_target_pairs={{0,1},{1,0},{2,3},{3,2},{4,5},{5,4},{6,7},{7,6},{8,9},{9,8},{10,11... | collective-permute-start | bytes 1966088 | tf_op jit(solution)/shard_map/ppermute | solution.py:461
  458.0 16.7 %collective-permute-start.51 = (bf16[4,80,1024]{2,1,0:T(8,128)(2,1)S(1)}, bf16[4,80,1024]{2,1,0:T(8,128)(2,1)S(1)}, u32[]{:S(2)}, u32[]{:S(2)}) collective-permute-start(bf16[4,80,1024]{2,1,0:T(8,128)(2,1)S(1)} %pad_maximum_fusion.18), channel_id=1, source_target_pairs={{0,2},{2,0},{4,6},{6,4},{1,3},{3,1},{5,7},{7,5},{8,10},{10,8},{12,... | collective-permute-start | bytes 1966088 | tf_op jit(solution)/shard_map/ppermute | solution.py:461
  460.8 20.5 %collective-permute-start.45 = (bf16[4,96,1024]{2,1,0:T(8,128)(2,1)S(1)}, bf16[4,96,1024]{2,1,0:T(8,128)(2,1)S(1)}, u32[]{:S(2)}, u32[]{:S(2)}) collective-permute-start(bf16[4,96,1024]{2,1,0:T(8,128)(2,1)S(1)} %pad_maximum_fusion.13), channel_id=1, source_target_pairs={{0,4},{2,6},{4,0},{6,2},{1,5},{3,7},{5,1},{7,3},{8,12},{10,14},{12... | collective-permute-start | bytes 2359304 | tf_op jit(solution)/shard_map/ppermute | solution.py:461
  463.1 22.9 %collective-permute-start.63 = (f32[8,2048]{1,0:T(8,128)S(1)}, f32[8,2048]{1,0:T(8,128)S(1)}, u32[]{:S(2)}, u32[]{:S(2)}) collective-permute-start(f32[8,2048]{1,0:T(8,128)S(1)} %copy-done.21), channel_id=1, source_target_pairs={{0,16},{8,24},{16,0},{24,8},{1,17},{9,25},{17,1},{25,9},{2,18},{10... | collective-permute-start | bytes 196616 | tf_op jit(solution)/shard_map/ppermute | solution.py:461
  472.1 59.7 %collective-permute-start.37 = (bf16[2,2,128,1024]{3,2,1,0:T(8,128)(2,1)}, bf16[2,2,128,1024]{3,2,1,0:T(8,128)(2,1)}, u32[]{:S(2)}, u32[]{:S(2)}) collective-permute-start(bf16[2,2,128,1024]{3,2,1,0:T(8,128)(2,1)} %dynamic-slice_bitcast_fusion), channel_id=1, source_target_pairs={{0,4},{2,6},{4,0},{6,2},{1,5},{3,7},{5,1},{7,3},{8,12},{10,14},{12... | collective-permute-start | bytes 3145736 | tf_op jit(solution)/shard_map/ppermute | solution.py:461
  474.7 51.9 %collective-permute-start.20 = (bf16[2,80,1024]{2,1,0:T(8,128)(2,1)}, bf16[2,80,1024]{2,1,0:T(8,128)(2,1)}, u32[]{:S(2)}, u32[]{:S(2)}) collective-permute-start(bf16[2,80,1024]{2,1,0:T(8,128)(2,1)} %dynamic-slice_bitcast_fusion.4), channel_id=1, source_target_pairs={{0,1},{1,0},{2,3},{3,2},{4,5},{5,4},{6,7},{7,6},{8,9},{9,8},{10,11... | collective-permute-start | bytes 983048 | tf_op jit(solution)/shard_map/ppermute | solution.py:461
  481.3 53.7 %collective-permute-start.36 = (bf16[128,8,256]{2,0,1:T(8,128)(2,1)}, bf16[128,8,256]{2,0,1:T(8,128)(2,1)}, u32[]{:S(2)}, u32[]{:S(2)}) collective-permute-start(bf16[128,8,256]{2,0,1:T(8,128)(2,1)} %add_convert_fusion), channel_id=1, source_target_pairs={{0,16},{8,24},{16,0},{24,8},{1,17},{9,25},{17,1},{25,9},{2,18},{10... | collective-permute-start | bytes 1572872 | tf_op jit(solution)/shard_map/ppermute | solution.py:461
  485.4 44.5 %collective-permute-start.17 = (bf16[2,80,1024]{2,1,0:T(8,128)(2,1)}, bf16[2,80,1024]{2,1,0:T(8,128)(2,1)}, u32[]{:S(2)}, u32[]{:S(2)}) collective-permute-start(bf16[2,80,1024]{2,1,0:T(8,128)(2,1)} %dynamic-slice_bitcast_fusion.5), channel_id=1, source_target_pairs={{0,4},{2,6},{4,0},{6,2},{1,5},{3,7},{5,1},{7,3},{8,12},{10,14},{12... | collective-permute-start | bytes 983048 | tf_op jit(solution)/shard_map/ppermute | solution.py:461
  524.7 60.0 %collective-permute-start.64 = (bf16[4,1024,512]{2,1,0:T(8,128)(2,1)}, bf16[4,1024,512]{2,1,0:T(8,128)(2,1)}, u32[]{:S(2)}, u32[]{:S(2)}) collective-permute-start(bf16[4,1024,512]{2,1,0:T(8,128)(2,1)} %get-tuple-element.95), channel_id=1, source_target_pairs={{0,8},{8,0},{16,24},{24,16},{1,9},{9,1},{17,25},{25,17},{2,10},{10... | collective-permute-start | bytes 12582920 | tf_op jit(solution)/shard_map/ppermute | solution.py:461
  528.6 11.4 %collective-permute-start.21 = (bf16[80,1024]{1,0:T(8,128)(2,1)}, bf16[80,1024]{1,0:T(8,128)(2,1)}, u32[]{:S(2)}, u32[]{:S(2)}) collective-permute-start(bf16[80,1024]{1,0:T(8,128)(2,1)} %dynamic-slice_bitcast_fusion.8), channel_id=1, source_target_pairs={{0,2},{2,0},{4,6},{6,4},{1,3},{3,1},{5,7},{7,5},{8,10},{10,8},{12,... | collective-permute-start | bytes 491528 | tf_op jit(solution)/shard_map/ppermute | solution.py:461
  529.9 61.7 %collective-permute-start.65 = (bf16[4,1024,512]{2,1,0:T(8,128)(2,1)}, bf16[4,1024,512]{2,1,0:T(8,128)(2,1)}, u32[]{:S(2)}, u32[]{:S(2)}) collective-permute-start(bf16[4,1024,512]{2,1,0:T(8,128)(2,1)} %get-tuple-element.96), channel_id=1, source_target_pairs={{0,8},{8,0},{16,24},{24,16},{1,9},{9,1},{17,25},{25,17},{2,10},{10... | collective-permute-start | bytes 12582920 | tf_op jit(solution)/shard_map/ppermute | solution.py:461
  534.3 15.0 %collective-permute-start.38 = (bf16[2,128,1024]{2,1,0:T(8,128)(2,1)}, bf16[2,128,1024]{2,1,0:T(8,128)(2,1)}, u32[]{:S(2)}, u32[]{:S(2)}) collective-permute-start(bf16[2,128,1024]{2,1,0:T(8,128)(2,1)} %dynamic-slice_bitcast_fusion.2), channel_id=1, source_target_pairs={{0,2},{2,0},{4,6},{6,4},{1,3},{3,1},{5,7},{7,5},{8,10},{10,8},{12,... | collective-permute-start | bytes 1572872 | tf_op jit(solution)/shard_map/ppermute | solution.py:461
  535.1 63.4 %collective-permute-start.66 = (bf16[4,512,1024]{2,1,0:T(8,128)(2,1)}, bf16[4,512,1024]{2,1,0:T(8,128)(2,1)}, u32[]{:S(2)}, u32[]{:S(2)}) collective-permute-start(bf16[4,512,1024]{2,1,0:T(8,128)(2,1)} %get-tuple-element.97), channel_id=1, source_target_pairs={{0,8},{8,0},{16,24},{24,16},{1,9},{9,1},{17,25},{25,17},{2,10},{10... | collective-permute-start | bytes 12582920 | tf_op jit(solution)/shard_map/ppermute | solution.py:461
  540.1 17.2 %collective-permute-start.14 = (bf16[2,96,1024]{2,1,0:T(8,128)(2,1)}, bf16[2,96,1024]{2,1,0:T(8,128)(2,1)S(1)}, u32[]{:S(2)}, u32[]{:S(2)}) collective-permute-start(bf16[2,96,1024]{2,1,0:T(8,128)(2,1)} %dynamic-slice_bitcast_fusion.3), channel_id=1, source_target_pairs={{0,2},{2,0},{4,6},{6,4},{1,3},{3,1},{5,7},{7,5},{8,10},{10,8},{12,... | collective-permute-start | bytes 1179656 | tf_op jit(solution)/shard_map/ppermute | solution.py:461
  549.3 17.7 %collective-permute-start.18 = (bf16[80,1024]{1,0:T(8,128)(2,1)S(1)}, bf16[80,1024]{1,0:T(8,128)(2,1)S(1)}, u32[]{:S(2)}, u32[]{:S(2)}) collective-permute-start(bf16[80,1024]{1,0:T(8,128)(2,1)S(1)} %copy-done.19), channel_id=1, source_target_pairs={{0,1},{1,0},{2,3},{3,2},{4,5},{5,4},{6,7},{7,6},{8,9},{9,8},{10,11... | collective-permute-start | bytes 491528 | tf_op jit(solution)/shard_map/ppermute | solution.py:461
  557.2 7.9 %collective-permute-start.39 = (bf16[128,1024]{1,0:T(8,128)(2,1)S(1)}, bf16[128,1024]{1,0:T(8,128)(2,1)S(1)}, u32[]{:S(2)}, u32[]{:S(2)}) collective-permute-start(bf16[128,1024]{1,0:T(8,128)(2,1)S(1)} %dynamic-slice_bitcast_fusion.6), channel_id=1, source_target_pairs={{0,1},{1,0},{2,3},{3,2},{4,5},{5,4},{6,7},{7,6},{8,9},{9,8},{10,11... | collective-permute-start | bytes 786440 | tf_op jit(solution)/shard_map/ppermute | solution.py:461
  565.1 5.8 collective-permute-start.15
  571.0 12.8 %collective-permute-start.41 = (bf16[128,1024]{1,0:T(8,128)(2,1)S(1)}, bf16[128,1024]{1,0:T(8,128)(2,1)S(1)}, u32[]{:S(2)}, u32[]{:S(2)}) collective-permute-start(bf16[128,1024]{1,0:T(8,128)(2,1)S(1)} %add_convert_fusion.2), channel_id=1, source_target_pairs={{0,16},{8,24},{16,0},{24,8},{1,17},{9,25},{17,1},{25,9},{2,18},{10... | collective-permute-start | bytes 786440 | tf_op jit(solution)/shard_map/ppermute | solution.py:461
  (31 other events, 308.3 us)
